TPU v7x, 32 devices: a whole 2x2x4 slice. The times are simulated.
32 devices in a mesh: ax: 8 (over z, y), az: 4 (over x, core).
Axes of the slice: x: 2, y: 2, z: 4, core: 2. Of those that a mesh axis runs over, the one named last changes fastest.
Arguments:
- density: float32 [32, 256, 256], P('ax', 'az'), may hold values from 0.5 to 2
- velocity: float32 [3, 32, 256, 256], P(None, 'ax', 'az'), may hold values from -12 to 12
Outputs:
- stress_flux: float32 [3, 32, 256, 256], P(None, 'ax', 'az')
- coefficient: float32 [32, 256], P('ax')
All inputs are finite; a program needn't handle non-finite values.
Results may differ from a plain program's by a relative error of at most 0.00002.
Values sent between devices are 32-bit elements; how exact they have to be, the bound alone decides.
A program may use at most 64 MiB of HBM per device.

v0:
```python
import functools
import math

import jax
import jax.numpy as jnp
import numpy as np
from jax import lax
from jax.experimental import pallas as pl
from jax.experimental.pallas import tpu as pltpu
from jax.sharding import PartitionSpec as P

STEP_AXIAL = 0.5
STEP_RADIAL = 0.25
INNER_RADIUS = 10.0
FILTER_RATIO = 2.0
TINY = 1e-06
PAIRS = ((0, 0), (1, 1), (2, 2), (0, 1), (0, 2), (1, 2))
LANES = 128
SUB = 8
BLOCKS = {"first": 10, "hat": 10, "model": 10, "closure": 8, "flux": 8}
EDGE = 16
MESH_ID = pl.DeviceIdType.MESH


def geometry(radial, azimuth_cells):
    radius = INNER_RADIUS + (np.arange(radial, dtype=np.float64) + 0.5) * STEP_RADIAL
    angle = 2.0 * math.pi / azimuth_cells
    width = (STEP_AXIAL * STEP_RADIAL * angle * radius) ** (2.0 / 3.0)
    rows = np.stack(
        [
            1.0 / radius,
            0.5 / (radius * angle),
            width,
            FILTER_RATIO**2 * width,
            radius,
            0.5 / STEP_RADIAL / radius,
            radius * radius,
            0.5 / STEP_RADIAL / (radius * radius),
        ]
    ).astype(np.float32)
    rows = rows.reshape(rows.shape[0], radial // LANES, 1, LANES)
    return np.ascontiguousarray(np.broadcast_to(rows, rows.shape[:2] + (SUB, LANES)))


def before(x):
    lane = lax.broadcasted_iota(jnp.int32, x.shape, x.ndim - 1)
    y = pltpu.roll(x, 1, x.ndim - 1)
    fill = jnp.concatenate([x[:1], y[:-1]], axis=0)
    return jnp.where(lane == 0, fill, y)


def after(x):
    lane = lax.broadcasted_iota(jnp.int32, x.shape, x.ndim - 1)
    y = pltpu.roll(x, LANES - 1, x.ndim - 1)
    fill = jnp.concatenate([y[1:], x[-1:]], axis=0)
    return jnp.where(lane == LANES - 1, fill, y)


def rise(x):
    return after(x) - before(x)


def strain(dx, dr, dt, ur, ut, inv_r):
    s_xx, s_rr = dx[0], dr[1]
    s_tt = dt[2] + ur * inv_r
    s_xr = 0.5 * (dr[0] + dx[1])
    s_xt = 0.5 * (dt[0] + dx[2])
    s_rt = 0.5 * (dt[1] + dr[2] - ut * inv_r)
    size = jnp.sqrt(
        2.0
        * (
            s_xx * s_xx
            + s_rr * s_rr
            + s_tt * s_tt
            + 2.0 * (s_xr * s_xr + s_xt * s_xt + s_rt * s_rt)
        )
    )
    third = (s_xx + s_rr + s_tt) * (1.0 / 3.0)
    return (s_xx - third, s_rr - third, s_tt - third, s_xr, s_xt, s_rt), size


def kernel(
    n_ax, n_az, nx, nt, nh, relays,
    rho_ref, vel_ref, geo_ref, flux_ref, coef_ref,
    S, M, H, V, HM, PX, MX, ACC, part, rec, rec_lo, rec_hi, CS, R, LE,
    own_sem, halo_send, halo_recv, corner_send, corner_recv, sum_send, sum_recv,
    relay_send, relay_recv, pass_send,
):
    me_ax, me_az = lax.axis_index("ax"), lax.axis_index("az")
    left, right = lax.rem(me_az + n_az - 1, n_az), lax.rem(me_az + 1, n_az)
    has_lo, has_hi = me_ax > 0, me_ax < n_ax - 1
    azimuth_cells = nt * n_az

    own = []
    for h in range(nh):
        lanes = pl.ds(h * LANES, LANES)
        cols = pl.ds(EDGE, nt)
        own.append(pltpu.make_async_copy(
            rho_ref.at[:, :, lanes], S.at[0, pl.ds(2, nx), h, cols, :], own_sem.at[2 * h]))
        own.append(pltpu.make_async_copy(
            vel_ref.at[:, :, :, lanes], S.at[pl.ds(1, 3), pl.ds(2, nx), h, cols, :], own_sem.at[2 * h + 1]))
    for c in own:
        c.start()

    barrier = pltpu.get_barrier_semaphore()

    def greet(ax, az):
        pl.semaphore_signal(barrier, inc=1, device_id=(ax, az), device_id_type=MESH_ID)

    for d in range(1, n_az):
        greet(me_ax, lax.rem(me_az + d, n_az))

    @pl.when(has_lo)
    def _():
        for d in range(n_az):
            greet(me_ax - 1, lax.rem(me_az + d, n_az))

    @pl.when(has_hi)
    def _():
        for d in range(n_az):
            greet(me_ax + 1, lax.rem(me_az + d, n_az))

    peers = n_az - 1 + jnp.where(has_lo, n_az, 0) + jnp.where(has_hi, n_az, 0)
    if relays:
        @pl.when(me_ax > 1)
        def _():
            greet(me_ax - 2, me_az)

        @pl.when(me_ax < n_ax - 2)
        def _():
            greet(me_ax + 2, me_az)

        peers = peers + jnp.where(me_ax > 1, 1, 0) + jnp.where(me_ax < n_ax - 2, 1, 0)
    pl.semaphore_wait(barrier, peers)

    def halo(kind, src_rows, src_cols, dst_rows, dst_cols, target):
        copies = []
        for h in range(nh):
            lanes = pl.ds(h * LANES, LANES)
            copies.append(pltpu.make_async_remote_copy(
                src_ref=rho_ref.at[src_rows, src_cols, lanes],
                dst_ref=S.at[0, dst_rows, h, dst_cols, :],
                send_sem=halo_send.at[kind, 2 * h], recv_sem=halo_recv.at[kind, 2 * h],
                device_id=target, device_id_type=MESH_ID))
            copies.append(pltpu.make_async_remote_copy(
                src_ref=vel_ref.at[:, src_rows, src_cols, lanes],
                dst_ref=S.at[pl.ds(1, 3), dst_rows, h, dst_cols, :],
                send_sem=halo_send.at[kind, 2 * h + 1], recv_sem=halo_recv.at[kind, 2 * h + 1],
                device_id=target, device_id_type=MESH_ID))
        return copies

    def planes(kind, src, dst, target):
        def cells(at, rows, first, count):
            return halo(kind + at, pl.ds(src + rows[0], rows[1]), pl.ds(first, count),
                        pl.ds(dst + rows[0], rows[1]), pl.ds(EDGE + first, count), target)

        near_row = nx - 1 - src if src else 0
        return (
            cells(0, (0, 2), 0, SUB) + cells(1, (0, 2), nt - SUB, SUB),
            cells(2, (near_row, 1), SUB, span),
            cells(3, (near_row, 1), SUB + span, span),
            cells(4, (1 - near_row, 1), SUB, span),
            cells(5, (1 - near_row, 1), SUB + span, span),
        )

    span = nt // 2 - SUB
    up = planes(0, nx - 2, 0, (me_ax + 1, me_az))
    down = planes(6, 0, nx + 2, (me_ax - 1, me_az))
    around = halo(12, pl.ds(0, nx), pl.ds(nt - SUB, SUB), pl.ds(2, nx), pl.ds(EDGE - SUB, SUB), (me_ax, right))
    around += halo(13, pl.ds(0, nx), pl.ds(0, SUB), pl.ds(2, nx), pl.ds(EDGE + nt, SUB), (me_ax, left))

    pair, odd = me_ax // 2, lax.rem(me_ax, 2)
    is_odd, is_even = odd == 1, odd == 0
    rank_of = {5: 0, 4: 1, 3: 2}
    sent = jnp.where(is_odd, n_ax // 2 - 1 - pair, pair)
    passed = jnp.where(is_odd, pair, n_ax // 2 - 1 - pair)

    def relay(piece):
        rank, copies = rank_of[piece], []
        row = jnp.where(is_odd, nx - 1, 0) if piece == 3 else jnp.where(is_odd, nx - 2, 1)
        first = SUB + (0 if piece == 4 else span)
        to = (me_ax + 1 - 2 * odd, me_az)
        on = (me_ax + 2 - 4 * odd, me_az)
        land = jnp.where(is_odd, nx + 2, 1) if piece == 3 else jnp.where(is_odd, nx + 3, 0)
        kind = piece + 6 * odd
        onward = []
        for h in range(nh):
            lanes = pl.ds(h * LANES, LANES)
            for q, src, lead in (
                (2 * h, rho_ref.at[pl.ds(row, 1), pl.ds(first, span), lanes], 0),
                (2 * h + 1, vel_ref.at[:, pl.ds(row, 1), pl.ds(first, span), lanes], pl.ds(1, 3)),
            ):
                copies.append(pltpu.make_async_remote_copy(
                    src_ref=src, dst_ref=R.at[rank, lead, :, h],
                    send_sem=relay_send.at[rank, q], recv_sem=relay_recv.at[rank, q],
                    device_id=to, device_id_type=MESH_ID))
                onward.append(pltpu.make_async_remote_copy(
                    src_ref=R.at[rank, lead, :, h],
                    dst_ref=S.at[lead, pl.ds(land, 1), h, pl.ds(EDGE + first, span), :],
                    send_sem=pass_send.at[rank, q], recv_sem=halo_recv.at[kind, q],
                    device_id=on, device_id_type=MESH_ID))
        return copies, onward

    relayed = {piece: relay(piece) for piece in rank_of} if relays else {}

    def sends_up(piece):
        return has_hi & (is_even | (sent <= rank_of[piece])) if piece in relayed else has_hi

    def sends_down(piece):
        return has_lo & (is_odd | (sent <= rank_of[piece])) if piece in relayed else has_lo

    def send_relay(piece):
        if piece in relayed:
            @pl.when(sent > rank_of[piece])
            def _():
                for c in relayed[piece][0]:
                    c.start()

    def pass_on(piece):
        if piece in relayed:
            @pl.when(passed > rank_of[piece])
            def _():
                for got, c in zip(*relayed[piece]):
                    got.wait_recv()
                    c.start()

    for piece in range(5 + 1):
        at = max(piece - 1, 0)
        if piece == 1:
            for c in around:
                c.start()
            continue
        if piece == 3:
            send_relay(3)
        if piece == 4:
            send_relay(4)
            send_relay(5)

        @pl.when(sends_up(piece))
        def _():
            for c in up[at]:
                c.start()

        @pl.when(sends_down(piece))
        def _():
            for c in down[at]:
                c.start()

    def corner(slot, row):
        rows = pl.ds(row, 2)
        return [
            pltpu.make_async_remote_copy(
                src_ref=S.at[:, rows, :, pl.ds(EDGE + nt - SUB, SUB), :],
                dst_ref=S.at[:, rows, :, pl.ds(EDGE - SUB, SUB), :],
                send_sem=corner_send.at[slot, 0], recv_sem=corner_recv.at[slot, 0],
                device_id=(me_ax, right), device_id_type=MESH_ID),
            pltpu.make_async_remote_copy(
                src_ref=S.at[:, rows, :, pl.ds(EDGE, SUB), :],
                dst_ref=S.at[:, rows, :, pl.ds(EDGE + nt, SUB), :],
                send_sem=corner_send.at[slot, 1], recv_sem=corner_recv.at[slot, 1],
                device_id=(me_ax, left), device_id_type=MESH_ID),
        ]

    lo_corner, hi_corner = corner(0, 0), corner(1, nx + 2)

    def groups(flow):
        return flow[0], flow[1] + flow[2], flow[3] + flow[4]

    def receive(step):
        @pl.when(has_lo)
        def _():
            for c in groups(up)[step]:
                c.wait_recv()
            for c in lo_corner:
                c.start() if step == 0 else c.wait() if step == 1 else None

        @pl.when(has_hi)
        def _():
            for c in groups(down)[step]:
                c.wait_recv()
            for c in hi_corner:
                c.start() if step == 0 else c.wait() if step == 1 else None

    def low(r):
        return jnp.maximum(r - 1, jnp.where(has_lo, -2, 0))

    def high(r):
        return jnp.minimum(r + 1, jnp.where(has_hi, nx + 1, nx - 1))

    def sweep(first, stride, count, tiles, body):
        tiles = tiles // body.size

        def step(at, carry):
            r = first + stride * (at // tiles)
            body(r, lax.rem(at, tiles))
            return carry

        lax.fori_loop(0, count * tiles, step, 0)

    wide = nt // SUB + 2

    def blocked(name, extent):
        size = math.gcd(BLOCKS[name], extent)

        def mark(body):
            body.size = size
            return body

        return size * SUB, mark

    def spread(values, rows):
        return jnp.concatenate([values] * (rows // SUB), axis=1)

    def near(ref, lead, row, col, shift, n):
        return ref[lead, row, :, pl.ds(col + shift, n), :]

    def tile(ref, lead, row, col, n):
        return ref[lead, row, :, pl.ds(pl.multiple_of(col, SUB), n), :]

    def put(ref, lead, row, col, value):
        ref[lead, row, :, pl.ds(pl.multiple_of(col, SUB), value.shape[1]), :] = value

    def first_pass(with_pairs):
        n, mark = blocked("first", wide)

        @mark
        def body(r, t):
            c = (EDGE - SUB) + t * n
            rows = (low(r) + 2, r + 2, high(r) + 2)
            rho = [tile(S, 0, q, c, n) for q in rows]
            vel = [[tile(S, 1 + a, q, c, n) for a in range(3)] for q in rows]
            inv_r, az_scale, width = (spread(geo_ref[g], n) for g in (0, 1, 2))
            dx = [vel[2][a] - vel[0][a] for a in range(3)]
            dr = [rise(vel[1][a]) * (0.5 / STEP_RADIAL) for a in range(3)]
            dt = [(near(S, 1 + a, r + 2, c, 1, n) - near(S, 1 + a, r + 2, c, -1, n)) * az_scale for a in range(3)]
            dev, size = strain(dx, dr, dt, vel[1][1], vel[1][2], inv_r)
            scale = rho[1] * width * size
            for a in range(6):
                put(M, a, r + 1, c, scale * dev[a])
            mom = [[rho[q] * vel[q][a] for a in range(3)] for q in range(3)]
            put(H, 0, r + 1, c, (rho[0] + rho[1]) + (rho[1] + rho[2]))
            for a in range(3):
                put(H, 1 + a, r + 1, c, (mom[0][a] + mom[1][a]) + (mom[1][a] + mom[2][a]))
            if with_pairs:
                for at, (a, b) in enumerate(PAIRS):
                    p = [mom[q][a] * vel[q][b] for q in range(3)]
                    put(PX, at, r, c, (p[0] + p[1]) + (p[1] + p[2]))
        return body

    def smooth(ref, lead, row, c, n):
        mid_value = tile(ref, lead, row, c, n)
        s = (near(ref, lead, row, c, -1, n) + near(ref, lead, row, c, 1, n)) + (mid_value + mid_value)
        return ((before(s) + after(s)) + (s + s)) * (1.0 / 64.0)

    n_hat, mark_hat = blocked("hat", wide)

    @mark_hat
    def hat_pass(r, t):
        n = n_hat
        c = (EDGE - SUB) + t * n
        hat = [smooth(H, a, r + 1, c, n) for a in range(4)]
        inv = 1.0 / hat[0]
        for a in range(4):
            put(HM, a, r + 1, c, hat[a])
        for a in range(3):
            put(V, a, r + 1, c, hat[1 + a] * inv)

    n_model, mark_model = blocked("model", wide)

    @mark_model
    def model_pass(r, t):
        n = n_model
        c = (EDGE - SUB) + t * n
        for a in range(6):
            m = tile(M, a, r + 1, c, n)
            put(MX, a, r, c, (tile(M, a, low(r) + 1, c, n) + m) + (m + tile(M, a, high(r) + 1, c, n)))

    n_leonard, mark_leonard = blocked("closure", nt // SUB)

    @mark_leonard
    def leonard_pass(r, t):
        n = n_leonard
        c = EDGE + t * n
        hv = [tile(V, a, r + 1, c, n) for a in range(3)]
        hm = [tile(HM, 1 + a, r + 1, c, n) for a in range(3)]
        for at, (a, b) in enumerate(PAIRS):
            put(LE, at, r, c, smooth(PX, at, r, c, n) - hm[a] * hv[b])

    n_closure, mark_closure = blocked("closure", nt // SUB)

    @mark_closure
    def closure_pass(r, t):
        n = n_closure
        c = EDGE + t * n
        inv_r, az_scale, width4 = (spread(geo_ref[g], n) for g in (0, 1, 3))
        hv = [tile(V, a, r + 1, c, n) for a in range(3)]
        dx = [tile(V, a, high(r) + 1, c, n) - tile(V, a, low(r) + 1, c, n) for a in range(3)]
        dr = [rise(hv[a]) * (0.5 / STEP_RADIAL) for a in range(3)]
        dt = [(near(V, a, r + 1, c, 1, n) - near(V, a, r + 1, c, -1, n)) * az_scale for a in range(3)]
        dev, size = strain(dx, dr, dt, hv[1], hv[2], inv_r)
        scale = width4 * tile(HM, 0, r + 1, c, n) * size
        lm, mm = [], []
        for at in range(6):
            mixed = scale * dev[at] - smooth(MX, at, r, c, n)
            leonard = tile(LE, at, r, c, n)
            lm.append(leonard * mixed)
            mm.append(mixed * mixed)
        for q, terms in enumerate((lm, mm)):
            cells = (terms[0] + terms[1] + terms[2]) + 2.0 * (terms[3] + terms[4] + terms[5])
            ACC[r, q] += sum(cells[:, s:s + SUB] for s in range(0, n, SUB))

    ACC[...] = jnp.zeros_like(ACC)
    for c in own:
        c.wait()
    for c in around:
        c.wait_recv()
    sweep(1, 1, nx - 2, wide, first_pass(True))
    sweep(1, 1, nx - 2, wide, hat_pass)
    receive(0)
    pass_on(3)
    receive(1)
    pass_on(4)
    sweep(0, nx - 1, 2, wide, first_pass(True))
    sweep(0, nx - 1, 2, wide, hat_pass)
    pass_on(5)
    sweep(0, 1, nx, nt // SUB, leonard_pass)
    sweep(1, 1, nx - 2, wide, model_pass)
    sweep(1, 1, nx - 2, nt // SUB, closure_pass)
    receive(2)
    sweep(-1, nx + 1, 2, wide, first_pass(False))
    sweep(-1, nx + 1, 2, wide, hat_pass)
    sweep(0, nx - 1, 2, wide, model_pass)
    sweep(0, nx - 1, 2, nt // SUB, closure_pass)

    for r in range(nx):
        for q in range(2):
            for h in range(nh):
                row = jnp.sum(ACC[r, q, h], axis=0, keepdims=True)
                part[r, pl.ds(q * nh + h, 1), :] = row
                rec[me_az, r, pl.ds(q * nh + h, 1), :] = row

    def share(kind, d, src, dst, ax):
        return pltpu.make_async_remote_copy(
            src_ref=src, dst_ref=dst.at[me_az],
            send_sem=sum_send.at[kind, d], recv_sem=sum_recv.at[kind, d],
            device_id=(ax, lax.rem(me_az + d, n_az)), device_id_type=MESH_ID)

    to_hi = [share(1, d, part.at[nx - 1], rec_lo, me_ax + 1) for d in range(n_az)]
    to_lo = [share(2, d, part.at[0], rec_hi, me_ax - 1) for d in range(n_az)]
    across = [share(0, d, part, rec, me_ax) for d in range(1, n_az)]

    @pl.when(has_hi)
    def _():
        for c in to_hi:
            c.start()

    @pl.when(has_lo)
    def _():
        for c in to_lo:
            c.start()

    for c in across:
        c.start()

    def ratio(sums):
        lm, mm = sums[:nh], sums[nh:]
        return -0.5 * (lm * (1.0 / azimuth_cells)) / (mm * (1.0 / azimuth_cells) + TINY)

    def total(ref):
        sums = ref[0]
        for d in range(1, n_az):
            sums = sums + ref[d]
        return sums

    def keep(row, value):
        for h in range(nh):
            CS[row, h] = jnp.broadcast_to(-2.0 * value[h:h + 1], (SUB, LANES))

    for c in across:
        c.wait_recv()
    for r in range(nx):
        value = ratio(total(rec.at[:, r]))
        keep(r + 1, value)
        for h in range(nh):
            coef_ref[pl.ds(r, 1), pl.ds(h * LANES, LANES)] = value[h:h + 1]

    n_flux, mark_flux = blocked("flux", nt // SUB)

    @mark_flux
    def flux_pass(r, t):
        n = n_flux
        c = EDGE + t * n
        inv_r, az_scale, radius, back, radius2, back2 = (spread(geo_ref[g], n) for g in (0, 1, 4, 5, 6, 7))
        lo, hi = low(r) + 1, high(r) + 1
        here, below, above = (spread(CS[q], n) for q in (r + 1, lo, hi))

        def axial(a):
            return above * tile(M, a, hi, c, n) - below * tile(M, a, lo, c, n)

        def around_of(a):
            return (near(M, a, r + 1, c, 1, n) - near(M, a, r + 1, c, -1, n)) * turn

        turn = here * az_scale
        once = here * radius
        d_xr = rise(once * tile(M, 3, r + 1, c, n)) * back
        d_rr = rise(once * tile(M, 1, r + 1, c, n)) * back
        d_rt = rise(here * radius2 * tile(M, 5, r + 1, c, n)) * back2
        out = (
            axial(0) + d_xr + around_of(4),
            axial(3) + d_rr + around_of(5) - here * tile(M, 2, r + 1, c, n) * inv_r,
            axial(4) + d_rt + around_of(2),
        )
        rows = pl.ds(pl.multiple_of(t * n, SUB), n)
        for a in range(3):
            for h in range(nh):
                flux_ref[a, r, rows, pl.ds(h * LANES, LANES)] = out[a][h]

    sweep(1, 1, nx - 2, nt // SUB, flux_pass)

    @pl.when(has_lo)
    def _():
        for c in to_hi:
            c.wait_recv()
        keep(0, ratio(total(rec_lo)))

    @pl.when(has_hi)
    def _():
        for c in to_lo:
            c.wait_recv()
        keep(nx + 1, ratio(total(rec_hi)))

    sweep(0, nx - 1, 2, nt // SUB, flux_pass)

    for c in across + around:
        c.wait_send()

    for piece in (0, 2, 3, 4, 5):
        at = max(piece - 1, 0)

        @pl.when(sends_up(piece))
        def _():
            for c in up[at]:
                c.wait_send()

        @pl.when(sends_down(piece))
        def _():
            for c in down[at]:
                c.wait_send()

    for piece, (copies, onward) in relayed.items():
        @pl.when(sent > rank_of[piece])
        def _():
            for c in copies:
                c.wait_send()

        @pl.when(passed > rank_of[piece])
        def _():
            for c in onward:
                c.wait_send()

    @pl.when(has_hi)
    def _():
        for c in to_hi:
            c.wait_send()

    @pl.when(has_lo)
    def _():
        for c in to_lo:
            c.wait_send()


def hand_over(flux_in, coef_in, flux_out, coef_out, flux_buf, coef_buf, sems):
    count = flux_in.shape[0]
    pieces = [(flux_in.at[a], flux_buf.at[a], flux_out.at[a]) for a in range(count)]
    pieces.append((coef_in, coef_buf, coef_out))
    take = [pltpu.make_async_copy(a, b, sems.at[0, at]) for at, (a, b, _) in enumerate(pieces)]
    give = [pltpu.make_async_copy(b, c, sems.at[1, at]) for at, (_, b, c) in enumerate(pieces)]
    for c in take:
        c.start()
    for arrive, leave in zip(take, give):
        arrive.wait()
        leave.start()
    for c in give:
        c.wait()


def shards(n_ax, n_az, density, velocity):
    nx, nt, radial = density.shape
    nh = radial // LANES
    cols = nt + 2 * EDGE
    relays = n_ax == 8
    geo = jnp.asarray(geometry(radial, nt * n_az))

    def field(count, rows):
        return pltpu.VMEM((count, rows, nh, cols, LANES), jnp.float32)

    dma = pltpu.SemaphoreType.DMA
    flux, coef = pl.pallas_call(
        functools.partial(kernel, n_ax, n_az, nx, nt, nh, relays),
        out_shape=(
            jax.ShapeDtypeStruct(velocity.shape, jnp.float32),
            jax.ShapeDtypeStruct((nx, radial), jnp.float32),
        ),
        in_specs=[
            pl.BlockSpec(memory_space=pl.ANY),
            pl.BlockSpec(memory_space=pl.ANY),
            pl.BlockSpec(memory_space=pltpu.VMEM),
        ],
        out_specs=(
            pl.BlockSpec(memory_space=pltpu.VMEM),
            pl.BlockSpec(memory_space=pltpu.VMEM),
        ),
        scratch_shapes=[
            field(4, nx + 4),
            field(6, nx + 2),
            field(4, nx + 2),
            field(3, nx + 2),
            field(4, nx + 2),
            field(6, nx),
            field(6, nx),
            pltpu.VMEM((nx, 2, nh, SUB, LANES), jnp.float32),
            pltpu.VMEM((nx, 2 * nh, LANES), jnp.float32),
            pltpu.VMEM((n_az, nx, 2 * nh, LANES), jnp.float32),
            pltpu.VMEM((n_az, 2 * nh, LANES), jnp.float32),
            pltpu.VMEM((n_az, 2 * nh, LANES), jnp.float32),
            pltpu.VMEM((nx + 2, nh, SUB, LANES), jnp.float32),
            pltpu.VMEM((3, 4, 1, nh, nt // 2 - SUB, LANES), jnp.float32),
            field(6, nx),
            dma((2 * nh,)),
            dma((14, 2 * nh)),
            dma((14, 2 * nh)),
            dma((2, 2)),
            dma((2, 2)),
            dma((3, n_az)),
            dma((3, n_az)),
            dma((3, 2 * nh)),
            dma((3, 2 * nh)),
            dma((3, 2 * nh)),
        ],
        compiler_params=pltpu.CompilerParams(collective_id=0, has_side_effects=True),
        name="closure",
    )(density, velocity, geo)
    anywhere = pl.BlockSpec(memory_space=pl.ANY)
    return pl.pallas_call(
        hand_over,
        out_shape=(
            jax.ShapeDtypeStruct(flux.shape, jnp.float32),
            jax.ShapeDtypeStruct(coef.shape, jnp.float32),
        ),
        in_specs=[anywhere, anywhere],
        out_specs=(anywhere, anywhere),
        scratch_shapes=[
            pltpu.VMEM(flux.shape, jnp.float32),
            pltpu.VMEM(coef.shape, jnp.float32),
            dma((2, flux.shape[0] + 1)),
        ],
        name="hand_over",
    )(flux, coef)


def solution(mesh):
    in_specs = (P("ax", "az", None), P(None, "ax", "az", None))
    out_specs = (P(None, "ax", "az", None), P("ax", None))
    body = functools.partial(shards, mesh.shape["ax"], mesh.shape["az"])
    return jax.shard_map(body, mesh=mesh, in_specs=in_specs, out_specs=out_specs, check_vma=False)
```

profile of v0, /device:TPU:0, one launch (start us, length us, event | category | flops | bytes accessed | tf_op | source)
XLA Modules:
  0.0 38.0 jit_solution(14557352238024562336)
XLA Ops:
  0.6 35.4 %closure.1 = (f32[3,4,64,256]{3,2,1,0:T(8,128)}, f32[4,256]{1,0:T(4,128)}) custom-call(f32[4,64,256]{2,1,0:T(8,128)} %rho_ref.1, f32[3,4,64,256]{3,2,1,0:T(8,128)} %vel_ref.1, f32[8,2,8,128]{3,2,1,0:T(8,128)} %constant.2.clone.geo_ref), custom_call_target="tpu_custom_call" | custom-call | tf_op jit(solution)/shard_map/closure/pallas_call | solution.py:598
  36.1 1.9 %hand_over.1 = (f32[3,4,64,256]{3,2,1,0:T(8,128)}, f32[4,256]{1,0:T(4,128)}) custom-call(f32[3,4,64,256]{3,2,1,0:T(8,128)} %get-tuple-element.4.flux_in, f32[4,256]{1,0:T(4,128)} %get-tuple-element.5.coef_in), custom_call_target="tpu_custom_call" | custom-call | tf_op jit(solution)/shard_map/hand_over/pallas_call | solution.py:644
where the time goes:
time: 38.2 us; the launch traced here: 38 us
  Pallas kernels  37.3 us (98%)
  between operations  0.64 us (2%)
    pallas_call x1, Pallas kernels, shards(): pl.pallas_call(functools.partial(kernel, n_ax, n_az, nx, nt, nh, relays),...  35.4 us
    pallas_call x1, Pallas kernels, shards(): pl.pallas_call(hand_over, out_shape=(jax.ShapeDtypeStruct(flux.shape, jnp...  1.9 us

commit v1 on v0

v1 whole, which is shorter than its diff:
```python
import functools
import itertools
import math

import jax
import jax.numpy as jnp
import numpy as np
from jax import lax
from jax.experimental import pallas as pl
from jax.experimental.pallas import tpu as pltpu
from jax.sharding import PartitionSpec as P

STEP_AXIAL = 0.5
STEP_RADIAL = 0.25
INNER_RADIUS = 10.0
FILTER_RATIO = 2.0
TINY = 1e-06
PAIRS = ((0, 0), (0, 1), (0, 2), (1, 1), (2, 2), (1, 2))
DIAGONAL = (0, 3, 4)
CROSS = (1, 2, 5)
LANES = 128
SUB = 8
EDGE = 16
SEAM = 4
COPIES = 64
MESH_ID = pl.DeviceIdType.MESH


def geometry(radial, azimuth_cells):
    radius = INNER_RADIUS + (np.arange(radial, dtype=np.float64) + 0.5) * STEP_RADIAL
    angle = 2.0 * math.pi / azimuth_cells
    width = (STEP_AXIAL * STEP_RADIAL * angle * radius) ** (2.0 / 3.0)
    rows = np.stack(
        [
            1.0 / radius,
            0.5 / (radius * angle),
            width,
            FILTER_RATIO**2 * width,
            radius,
            0.5 / STEP_RADIAL / radius,
            radius * radius,
            0.5 / STEP_RADIAL / (radius * radius),
        ]
    ).astype(np.float32)
    halves = rows.reshape(rows.shape[0], radial // LANES, 1, LANES)
    at_seam = radial // 2 - SEAM // 2 + np.arange(LANES) % SEAM
    seam = rows[:4, None, at_seam]
    return (
        np.ascontiguousarray(np.broadcast_to(halves, halves.shape[:2] + (SUB, LANES))),
        np.ascontiguousarray(np.broadcast_to(seam, (4, SUB, LANES))),
    )


def lane_of(x):
    return lax.broadcasted_iota(jnp.int32, x.shape, x.ndim - 1)


def before(x):
    y = pltpu.roll(x, 1, x.ndim - 1)
    fill = jnp.concatenate([x[:1], y[:-1]], axis=0)
    return jnp.where(lane_of(x) == 0, fill, y)


def after(x):
    y = pltpu.roll(x, LANES - 1, x.ndim - 1)
    fill = jnp.concatenate([y[1:], x[-1:]], axis=0)
    return jnp.where(lane_of(x) == LANES - 1, fill, y)


def rise(x):
    return after(x) - before(x)


def sides(x, end):
    lane = lane_of(x)
    return (
        jnp.where(lane == 0, end, pltpu.roll(x, 1, 1)),
        jnp.where(lane == LANES - 1, end, pltpu.roll(x, LANES - 1, 1)),
    )


def strain(dx, dr, dt, ur, ut, inv_r):
    s_xx, s_rr = dx[0], dr[1]
    s_tt = dt[2] + ur * inv_r
    s_xr = 0.5 * (dr[0] + dx[1])
    s_xt = 0.5 * (dt[0] + dx[2])
    s_rt = 0.5 * (dt[1] + dr[2] - ut * inv_r)
    size = jnp.sqrt(
        2.0
        * (
            s_xx * s_xx
            + s_rr * s_rr
            + s_tt * s_tt
            + 2.0 * (s_xr * s_xr + s_xt * s_xt + s_rt * s_rt)
        )
    )
    third = (s_xx + s_rr + s_tt) * (1.0 / 3.0)
    return (s_xx - third, s_xr, s_xt, s_rr - third, s_tt - third, s_rt), size


def kernel(
    n_ax, n_az, nx, nt,
    rho_ref, vel_ref, geo_ref, seam_ref, flux_ref, coef_ref,
    S, T, M, H, V, HM, PX, MX, E, G, GM, GH, GP, GX, GV,
    part, rec, rec_out, CS, own_sem, send_sem, recv_sem, sum_send, sum_recv,
):
    pr = 2 * nx
    me_ax, me_az = lax.axis_index("ax"), lax.axis_index("az")
    left, right = lax.rem(me_az + n_az - 1, n_az), lax.rem(me_az + 1, n_az)
    odd = lax.rem(me_ax, 2)
    even = 1 - odd
    mine, other = odd, even
    azimuth_cells = nt * n_az

    def pick(at_even, at_odd):
        return jnp.where(odd == 0, at_even, at_odd)

    has_lo, has_hi = me_ax > 0, me_ax < n_ax - 1
    pair_lo, pair_hi = me_ax >= 2, me_ax < n_ax - 2
    partner = me_ax + 1 - 2 * odd
    near_ax = me_ax - 2 + 4 * odd
    far_ax = me_ax + 2 - 4 * odd
    edge_ax = me_ax - 1 + 2 * odd
    has_near = (near_ax >= 0) & (near_ax < n_ax)
    has_far = (far_ax >= 0) & (far_ax < n_ax)

    lanes_mine = pl.ds(pl.multiple_of(mine * LANES, LANES), LANES)
    lanes_other = pl.ds(pl.multiple_of(other * LANES, LANES), LANES)
    cols = pl.ds(EDGE, nt)
    own_row = nx * odd
    own_at = own_row + 2
    partner_at = nx * even + 2
    near_at = pick(0, nx - 2)
    beyond_at = pick(pr + 2, 0)
    ahead_at = pick(0, pr + 2)
    pass_at = pick(pr, 2)

    own = [
        pltpu.make_async_copy(rho_ref.at[:, :, lanes_mine], S.at[0, pl.ds(own_at, nx), cols, :], own_sem.at[0]),
        pltpu.make_async_copy(
            vel_ref.at[:, :, :, lanes_mine], S.at[pl.ds(1, 3), pl.ds(own_at, nx), cols, :], own_sem.at[1]),
        pltpu.make_async_copy(rho_ref.at[:, :, lanes_other], T.at[0, pl.ds(1, nx), cols, :], own_sem.at[2]),
        pltpu.make_async_copy(
            vel_ref.at[:, :, :, lanes_other], T.at[pl.ds(1, 3), pl.ds(1, nx), cols, :], own_sem.at[3]),
    ]
    for c in own:
        c.start()

    barrier = pltpu.get_barrier_semaphore()

    def greet(ax, az):
        pl.semaphore_signal(barrier, inc=1, device_id=(ax, az), device_id_type=MESH_ID)

    for d in range(1, n_az):
        greet(me_ax, lax.rem(me_az + d, n_az))
    peers = n_az - 1
    for step in (-1, 1, -2, 2):
        there = (me_ax + step >= 0) & (me_ax + step < n_ax)

        @pl.when(there)
        def _():
            for d in range(n_az):
                greet(me_ax + step, lax.rem(me_az + d, n_az))

        peers = peers + jnp.where(there, n_az, 0)

    ids = itertools.count()

    def remote(src, dst, ax, az):
        at = next(ids)
        return pltpu.make_async_remote_copy(
            src_ref=src, dst_ref=dst, send_sem=send_sem.at[at], recv_sem=recv_sem.at[at],
            device_id=(ax, az), device_id_type=MESH_ID)

    def block(src_row, count, first, width, lanes, dst, dst_row, dst_first, ax, az):
        rows, at = pl.ds(src_row, count), pl.ds(first, width)
        to_rows, to = pl.ds(dst_row, count), pl.ds(dst_first, width)
        return [
            remote(rho_ref.at[rows, at, lanes], dst.at[0, to_rows, to, :], ax, az),
            remote(vel_ref.at[:, rows, at, lanes], dst.at[pl.ds(1, 3), to_rows, to, :], ax, az),
        ]

    def ends(src_row, count, lanes, dst, dst_row, ax, az):
        out = []
        for first in (0, nt - SUB):
            out += block(src_row, count, first, SUB, lanes, dst, dst_row, EDGE + first, ax, az)
        return out

    def middle(src_row, count, lanes, dst, dst_row, ax, az):
        return block(src_row, count, SUB, nt - 2 * SUB, lanes, dst, dst_row, EDGE + SUB, ax, az)

    def around(ref, lead, rows):
        at = (pl.ds(EDGE + nt - SUB, SUB), pl.ds(EDGE - SUB, SUB), pl.ds(EDGE, SUB), pl.ds(EDGE + nt, SUB))
        return [
            remote(ref.at[lead, rows, at[0], :], ref.at[lead, rows, at[1], :], me_ax, right),
            remote(ref.at[lead, rows, at[2], :], ref.at[lead, rows, at[3], :], me_ax, left),
        ]

    fold = nt // 2
    whole = pl.ds(SUB, fold)

    def seam_around(s):
        return [
            remote(E.at[s, pl.ds(fold, SUB), :], E.at[s, pl.ds(0, SUB), :], me_ax, right),
            remote(E.at[s, pl.ds(SUB, SUB), :], E.at[s, pl.ds(SUB + fold, SUB), :], me_ax, left),
        ]

    s_own, s_partner, s_beyond, s_ahead = 1 + odd, 2 - odd, pick(3, 0), pick(0, 3)

    own_around = []
    for lanes, dst, row in ((lanes_mine, S, own_at), (lanes_other, T, 1)):
        own_around += block(0, nx, nt - SUB, SUB, lanes, dst, row, EDGE - SUB, me_ax, right)
        own_around += block(0, nx, 0, SUB, lanes, dst, row, EDGE + nt, me_ax, left)
    seam_own = seam_around(s_own)
    seam_partner_around = seam_around(s_partner)
    seam_beyond_around = seam_around(s_beyond)
    seam_ahead_around = seam_around(s_ahead)

    seam_swap = remote(E.at[s_own, whole, :], E.at[s_own, whole, :], partner, me_az)
    seam_near = remote(E.at[s_own, whole, :], E.at[pick(3, 0), whole, :], near_ax, me_az)
    seam_pass = remote(E.at[s_partner, whole, :], E.at[pick(0, 3), whole, :], far_ax, me_az)

    swap_ends = ends(0, nx, lanes_other, S, own_at, partner, me_az)
    swap_rows = {}
    for q in range(nx):
        row = pick(nx - 1 - q, q)
        swap_rows[q] = middle(row, 1, lanes_other, S, own_at + row, partner, me_az)
    near_ends = ends(near_at, 2, lanes_mine, S, beyond_at, near_ax, me_az)
    near_rows = middle(near_at, 2, lanes_mine, S, beyond_at, near_ax, me_az)

    every = pl.ds(0, 4)

    def forward(row, first, width, count):
        return remote(
            S.at[:, pl.ds(pass_at + row, count), pl.ds(EDGE + first, width), :],
            S.at[:, pl.ds(ahead_at + row, count), pl.ds(EDGE + first, width), :], far_ax, me_az)

    pass_ends = [forward(0, first, SUB, 2) for first in (0, nt - SUB)]
    last_row = pick(1, 0)
    pass_rows = [forward(last_row, SUB, nt - 2 * SUB, 1), forward(1 - last_row, SUB, nt - 2 * SUB, 1)]
    partner_around = around(S, every, pl.ds(partner_at, nx))
    beyond_around = around(S, every, pl.ds(beyond_at, 2))
    ahead_around = around(S, every, pl.ds(ahead_at, 2))

    swap_row, edge_row = pick(nx - 1, 0), pick(0, nx - 1)
    three = pl.ds(1, 3)

    def flux_rows(row, dst_row, ax):
        return remote(
            vel_ref.at[:, pl.ds(row, 1), :, lanes_mine], T.at[three, pl.ds(dst_row, 1), cols, :], ax, me_az)

    def flux_stress(row, dst_row, ax):
        return remote(
            M.at[mine, pl.ds(0, 3), own_row + row + 1, cols, :], M.at[mine, pl.ds(0, 3), dst_row, cols, :],
            ax, me_az)

    swap_vel = flux_rows(swap_row, pick(0, nx + 1), partner)
    edge_vel = flux_rows(edge_row, pick(nx + 1, 0), edge_ax)
    swap_vel_around = around(T, three, pl.ds(pick(nx + 1, 0), 1))
    edge_vel_around = around(T, three, pl.ds(pick(0, nx + 1), 1))
    swap_stress = flux_stress(swap_row, pick(nx, nx + 1), partner)
    edge_stress = flux_stress(edge_row, pick(pr + 1, 0), edge_ax)

    def start(copies):
        for c in copies:
            c.start()

    def arrive(copies):
        for c in copies:
            c.wait_recv()

    def leave(copies):
        for c in copies:
            c.wait_send()

    wide = nt + 2 * SUB
    outer_cols = EDGE - SUB

    def lanes_at(n):
        return lax.broadcasted_iota(jnp.int32, (n, LANES), 1)

    def spread(values, rows):
        return jnp.concatenate([values] * (rows // SUB), axis=values.ndim - 2)

    def pack_seam():
        lane = lanes_at(nt)
        from_mine = jnp.where(lane >= LANES - SEAM // 2, 1, 0) == even
        half = lanes_at(fold)
        packed = jnp.zeros((fold, LANES), jnp.float32)
        for a in range(4):
            for i in range(nx):
                first = (a * nx + i) * SEAM
                x = jnp.where(from_mine, S[a, own_at + i, pl.ds(EDGE, nt), :], T[a, 1 + i, pl.ds(EDGE, nt), :])
                low = pltpu.roll(x[:fold], (first + SEAM // 2) % LANES, 1)
                high = pltpu.roll(x[fold:], (first + SEAM // 2 + LANES // 2) % LANES, 1)
                packed = jnp.where((half >= first) & (half < first + SEAM), low, packed)
                first += LANES // 2
                packed = jnp.where((half >= first) & (half < first + SEAM), high, packed)
        E[s_own, pl.ds(SUB, fold), :] = packed

    seam_lane = lanes_at(wide)
    seam_row = seam_lane // SEAM
    at_bottom = seam_row == jnp.where(pair_lo, -1, nx)
    at_top = seam_row == jnp.where(pair_hi, -1, nx + pr - 1)

    def seam_below(x):
        return jnp.where(at_bottom, x, pltpu.roll(x, SEAM, 1))

    def seam_above(x):
        return jnp.where(at_top, x, pltpu.roll(x, LANES - SEAM, 1))

    def seam_axial(x):
        return (seam_below(x) + x) + (x + seam_above(x))

    def seam_rise(x):
        return pltpu.roll(x, LANES - 1, 1) - pltpu.roll(x, 1, 1)

    span = pl.ds(outer_cols, wide)
    span_before, span_after = pl.ds(outer_cols - 1, wide), pl.ds(outer_cols + 1, wide)

    def seam_turn(ref, a):
        x = ref[a, span, :]
        return (ref[a, span_before, :] + ref[a, span_after, :]) + (x + x)

    def seam_pass_all():
        lane = lanes_at(fold + SUB)
        per = nx * SEAM
        for a in range(4):
            low = jnp.zeros((fold + SUB, LANES), jnp.float32)
            high = low
            for s in range(4):
                here = (lane >= s * per) & (lane < (s + 1) * per)
                x = pltpu.roll(E[s, pl.ds(SUB, fold + SUB), :], (s * per - a * per) % LANES, 1)
                low = jnp.where(here, x, low)
                x = pltpu.roll(E[s, pl.ds(0, fold + SUB), :], (s * per - a * per - LANES // 2) % LANES, 1)
                high = jnp.where(here, x, high)
            G[a, pl.ds(EDGE - SUB, SUB), :] = high[:SUB]
            G[a, pl.ds(EDGE, fold), :] = low[:fold]
            G[a, pl.ds(EDGE + fold, fold), :] = high[SUB:]
            G[a, pl.ds(EDGE + nt, SUB), :] = low[fold:]
        rho = G[0, span, :]
        vel = [G[1 + a, span, :] for a in range(3)]
        inv_r, az_scale, width = (spread(seam_ref[g], wide) for g in (0, 1, 2))
        dx = [seam_above(v) - seam_below(v) for v in vel]
        dr = [seam_rise(v) * (0.5 / STEP_RADIAL) for v in vel]
        dt = [(G[1 + a, span_after, :] - G[1 + a, span_before, :]) * az_scale for a in range(3)]
        dev, size = strain(dx, dr, dt, vel[1], vel[2], inv_r)
        scale = rho * width * size
        for a in range(6):
            GM[a, span, :] = seam_axial(scale * dev[a])
        mom = [rho * v for v in vel]
        GH[0, span, :] = seam_axial(rho)
        for a in range(3):
            GH[1 + a, span, :] = seam_axial(mom[a])
        for at, (a, b) in enumerate(PAIRS):
            GP[at, span, :] = seam_axial(mom[a] * vel[b])
        hat = []
        for a in range(4):
            s = seam_turn(GH, a)
            GX[a, span, :] = s
            hat.append(((pltpu.roll(s, 1, 1) + pltpu.roll(s, LANES - 1, 1)) + (s + s)) * (1.0 / 64.0))
        inv = 1.0 / hat[0]
        for a in range(3):
            GV[a, span, :] = hat[1 + a] * inv
        for a in range(6):
            GX[4 + a, span, :] = seam_turn(GP, a)
            GX[10 + a, span, :] = seam_turn(GM, a)

    end_lane = pick(LANES - 1, 0)

    def seam_end(x, ref, a, first, r):
        shift = pick(LANES - 1 - SEAM // 2, LANES - SEAM // 2 + 1) - SEAM * (r + nx)
        g = pltpu.roll(ref[a, pl.ds(first, x.shape[0]), :], shift, 1)
        return jnp.where(lane_of(x) == end_lane, g, x)

    def seam_slope(x, ref, a, first, r):
        lo, hi = sides(x, seam_end(x, ref, a, first, r))
        return hi - lo

    def smooth(ref, a, row, first, n, at, r):
        x = ref[a, row, pl.ds(first, n), :]
        s = (ref[a, row, pl.ds(first - 1, n), :] + ref[a, row, pl.ds(first + 1, n), :]) + (x + x)
        lo, hi = sides(s, seam_end(s, GX, at, first, r))
        return ((lo + hi) + (s + s)) * (1.0 / 64.0)

    def low(r):
        return jnp.maximum(r - 1, jnp.where(pair_lo, -2, 0))

    def high(r):
        return jnp.minimum(r + 1, jnp.where(pair_hi, pr + 1, pr - 1))

    def sweep(first, count, body):
        def step(at, carry):
            t = first + at
            body(pick(t, pr - 1 - t))
            return carry

        lax.fori_loop(0, count, step, 0)

    def turn_slope(ref, a, row, first, n):
        return ref[a, row, pl.ds(first + 1, n), :] - ref[a, row, pl.ds(first - 1, n), :]

    def first_pass(r, with_pairs):
        n, c = wide, outer_cols
        rows = (low(r) + 2, r + 2, high(r) + 2)
        rho = [S[0, q, pl.ds(c, n), :] for q in rows]
        vel = [[S[1 + a, q, pl.ds(c, n), :] for a in range(3)] for q in rows]
        inv_r, az_scale, width = (spread(geo_ref[g, mine], n) for g in (0, 1, 2))
        dx = [vel[2][a] - vel[0][a] for a in range(3)]
        dr = [seam_slope(vel[1][a], G, 1 + a, c, r) * (0.5 / STEP_RADIAL) for a in range(3)]
        dt = [turn_slope(S, 1 + a, r + 2, c, n) * az_scale for a in range(3)]
        dev, size = strain(dx, dr, dt, vel[1][1], vel[1][2], inv_r)
        scale = rho[1] * width * size
        for a in range(6):
            M[mine, a, r + 1, pl.ds(c, n), :] = scale * dev[a]
        mom = [[rho[q] * vel[q][a] for a in range(3)] for q in range(3)]
        H[0, r + 1, pl.ds(c, n), :] = (rho[0] + rho[1]) + (rho[1] + rho[2])
        for a in range(3):
            H[1 + a, r + 1, pl.ds(c, n), :] = (mom[0][a] + mom[1][a]) + (mom[1][a] + mom[2][a])
        if with_pairs:
            for at, (a, b) in enumerate(PAIRS):
                p = [mom[q][a] * vel[q][b] for q in range(3)]
                PX[at, r, pl.ds(c, n), :] = (p[0] + p[1]) + (p[1] + p[2])

    def hat_pass(r):
        n, c = wide, outer_cols
        hat = [smooth(H, a, r + 1, c, n, a, r) for a in range(4)]
        inv = 1.0 / hat[0]
        for a in range(4):
            HM[a, r + 1, pl.ds(c, n), :] = hat[a]
        for a in range(3):
            V[a, r + 1, pl.ds(c, n), :] = hat[1 + a] * inv

    def model_pass(r):
        n, c = wide, outer_cols
        for a in range(6):
            x = M[mine, a, r + 1, pl.ds(c, n), :]
            lo = M[mine, a, low(r) + 1, pl.ds(c, n), :]
            MX[a, r, pl.ds(c, n), :] = (lo + x) + (x + M[mine, a, high(r) + 1, pl.ds(c, n), :])

    def closure_pass(r):
        n, c = nt, EDGE
        inv_r, az_scale, width4 = (spread(geo_ref[g, mine], n) for g in (0, 1, 3))
        hv = [V[a, r + 1, pl.ds(c, n), :] for a in range(3)]
        hm = [HM[1 + a, r + 1, pl.ds(c, n), :] for a in range(3)]
        dx = [V[a, high(r) + 1, pl.ds(c, n), :] - V[a, low(r) + 1, pl.ds(c, n), :] for a in range(3)]
        dr = [seam_slope(hv[a], GV, a, c, r) * (0.5 / STEP_RADIAL) for a in range(3)]
        dt = [turn_slope(V, a, r + 1, c, n) * az_scale for a in range(3)]
        dev, size = strain(dx, dr, dt, hv[1], hv[2], inv_r)
        scale = width4 * HM[0, r + 1, pl.ds(c, n), :] * size
        lm, mm = [], []
        for at, (a, b) in enumerate(PAIRS):
            mixed = scale * dev[at] - smooth(MX, at, r, c, n, 10 + at, r)
            leonard = smooth(PX, at, r, c, n, 4 + at, r) - hm[a] * hv[b]
            lm.append(leonard * mixed)
            mm.append(mixed * mixed)
        for q, terms in enumerate((lm, mm)):
            diagonal, cross = (sum(terms[a] for a in group) for group in (DIAGONAL, CROSS))
            part[r, pl.ds(q, 1), :] = jnp.sum(diagonal + 2.0 * cross, axis=0, keepdims=True)

    def first_two(first, count, with_pairs=True):
        sweep(first, count, lambda r: first_pass(r, with_pairs))
        sweep(first, count, hat_pass)

    def close(first, count):
        sweep(first, count, model_pass)
        sweep(first, count, closure_pass)

    seam_far = pick(LANES - 1, 1)

    def other_half(i):
        n, c = wide, outer_cols
        inv_r, az_scale, width = (spread(geo_ref[g, other], n) for g in (0, 1, 2))
        lo = jnp.maximum(i - 1, jnp.where(has_lo, -1, 0)) + 1
        hi = jnp.minimum(i + 1, jnp.where(has_hi, nx, nx - 1)) + 1
        vel = [T[1 + a, i + 1, pl.ds(c, n), :] for a in range(3)]
        dx = [T[1 + a, hi, pl.ds(c, n), :] - T[1 + a, lo, pl.ds(c, n), :] for a in range(3)]
        dr = []
        for a in range(3):
            far = pltpu.roll(S[1 + a, own_at + i, pl.ds(c, n), :], pick(1, LANES - 1), 1)
            before_, after_ = sides(vel[a], jnp.where(lane_of(far) == pick(0, LANES - 1), far, vel[a]))
            dr.append((after_ - before_) * (0.5 / STEP_RADIAL))
        dt = [turn_slope(T, 1 + a, i + 1, c, n) * az_scale for a in range(3)]
        dev, size = strain(dx, dr, dt, vel[1], vel[2], inv_r)
        scale = T[0, i + 1, pl.ds(c, n), :] * width * size
        for a in range(6):
            M[other, a, own_row + i + 1, pl.ds(c, n), :] = scale * dev[a]

    def rows_of(first, count, body):
        def step(at, carry):
            body(first + at)
            return carry

        lax.fori_loop(0, count, step, 0)

    for c in own:
        c.wait()
    pack_seam()
    pl.semaphore_wait(barrier, peers)
    start([seam_swap] + swap_ends)
    start(seam_own + own_around)

    @pl.when(has_near)
    def _():
        start([seam_near] + near_ends + near_rows)

    for q in [nx - 1, nx - 2] + list(range(nx - 2)):
        start(swap_rows[q])
    swap_vel.start()

    seam_swap.wait_recv()
    start(seam_partner_around)

    @pl.when(has_far)
    def _():
        seam_pass.start()
        seam_near.wait_recv()
        start(seam_beyond_around)

    arrive(own_around)
    rows_of(1, nx - 2, other_half)

    @pl.when(has_near)
    def _():
        seam_pass.wait_recv()
        start(seam_ahead_around)

    arrive(swap_ends)
    start(partner_around)

    @pl.when(has_far)
    def _():
        start(pass_ends)
        arrive(near_ends)
        start(beyond_around)

    arrive(seam_own + seam_partner_around)

    @pl.when(has_far)
    def _():
        arrive(seam_beyond_around)

    @pl.when(has_near)
    def _():
        arrive(seam_ahead_around)

    seam_pass_all()
    first_two(1, nx - 2)

    @pl.when(has_near)
    def _():
        arrive(pass_ends)
        start(ahead_around)

    for at in range(2):
        arrive(swap_rows[nx - 1 - at])

        @pl.when(has_far)
        def _():
            pass_rows[at].start()

    @pl.when(has_far)
    def _():
        arrive(near_rows)
        arrive(beyond_around)

    arrive(partner_around)
    first_two(pr - 1, 1)
    first_two(pr, 1, False)
    for q in range(nx - 3):
        arrive(swap_rows[q])
        first_two(nx - 1 + q, 1)
        close(nx - 2 + q, 1)

    @pl.when(has_near)
    def _():
        edge_vel.start()
        arrive(pass_rows)
        arrive(ahead_around)

    first_two(-1, 1, False)
    first_two(0, 1)
    close(0, 2)
    arrive(swap_rows[nx - 3])
    swap_stress.start()

    @pl.when(has_near)
    def _():
        edge_stress.start()

    first_two(pr - 4, 3)
    close(pr - 5, 5)

    def share(at, src, dst, ax, d):
        return pltpu.make_async_remote_copy(
            src_ref=src, dst_ref=dst, send_sem=sum_send.at[at], recv_sem=sum_recv.at[at],
            device_id=(ax, lax.rem(me_az + d, n_az)), device_id_type=MESH_ID)

    def end_row(kind, half, row, ax):
        return [
            share((2 + 2 * kind + half) * n_az + d, part.at[row], rec_out.at[half, me_az], ax, d)
            for d in range(n_az)
        ]

    across = [share(d, part, rec.at[mine, me_az], me_ax, d) for d in range(1, n_az)]
    over = [share(n_az + d, part, rec.at[mine, me_az], partner, d) for d in range(n_az)]
    lower_ax, upper_ax = me_ax - odd - 1, me_ax - odd + 2
    down, up = end_row(0, mine, 0, lower_ax), end_row(1, mine, pr - 1, upper_ax)
    end_sums = end_row(even, 0, 0, me_ax) + end_row(even, 1, 0, me_ax)

    @pl.when(pair_lo)
    def _():
        start(down)

    @pl.when(pair_hi)
    def _():
        start(up)

    start(over)
    start(across)
    rec[mine, me_az] = part[...]
    swap_vel.wait_recv()
    start(swap_vel_around)

    @pl.when(has_near)
    def _():
        edge_vel.wait_recv()
        start(edge_vel_around)

    arrive(swap_vel_around)
    other_half(swap_row)

    @pl.when(has_near)
    def _():
        arrive(edge_vel_around)

    other_half(edge_row)

    def ratio(sums):
        lm, mm = sums[0:1], sums[1:2]
        return -0.5 * (lm * (1.0 / azimuth_cells)) / (mm * (1.0 / azimuth_cells) + TINY)

    def total(ref, h, row):
        terms = [ref[h, d] if row is None else ref[h, d, row] for d in range(n_az)]
        sums = terms[0]
        for x in terms[1:]:
            sums = sums + x
        return sums

    def keep(row, h, value):
        CS[row, h] = jnp.broadcast_to(-2.0 * value, (SUB, LANES))

    arrive(across)
    arrive(over)
    for i in range(nx + 1):
        row = i + even
        for h in range(2):
            keep(row, h, ratio(total(rec, h, own_row + row - 1)))
    for i in range(nx):
        for h in range(2):
            coef_ref[pl.ds(i, 1), pl.ds(h * LANES, LANES)] = -0.5 * CS[i + 1, h, pl.ds(0, 1), :]

    def flux_pass(i):
        n, c = nt, EDGE
        r = own_row + i + 1
        inv_r, az_scale, radius, back, radius2, back2 = (spread(geo_ref[g], n) for g in (0, 1, 4, 5, 6, 7))
        lo = jnp.maximum(i - 1, jnp.where(has_lo, -1, 0)) + 1
        hi = jnp.minimum(i + 1, jnp.where(has_hi, nx, nx - 1)) + 1
        here, below, above = (spread(CS[q], n) for q in (i + 1, lo, hi))

        def at(a, row, shift=0):
            return M[:, a, row, pl.ds(c + shift, n), :]

        def axial(a):
            return above * at(a, own_row + hi) - below * at(a, own_row + lo)

        def around_of(a):
            return (at(a, r, 1) - at(a, r, -1)) * turn

        turn = here * az_scale
        once = here * radius
        d_xr = rise(once * at(1, r)) * back
        d_rr = rise(once * at(3, r)) * back
        d_rt = rise(here * radius2 * at(5, r)) * back2
        out = (
            axial(0) + d_xr + around_of(2),
            axial(1) + d_rr + around_of(5) - here * at(4, r) * inv_r,
            axial(2) + d_rt + around_of(4),
        )
        for a in range(3):
            for h in range(2):
                flux_ref[a, i, :, pl.ds(h * LANES, LANES)] = out[a][h]

    rows_of(1, nx - 2, flux_pass)

    @pl.when(has_near)
    def _():
        arrive(end_sums)

    swap_stress.wait_recv()
    flux_pass(swap_row)

    @pl.when(has_near)
    def _():
        for h in range(2):
            keep(pick(0, nx + 1), h, ratio(total(rec_out, h, None)))
        edge_stress.wait_recv()

    flux_pass(edge_row)

    leave([seam_swap, swap_vel, swap_stress] + swap_ends + own_around + seam_own + seam_partner_around)
    leave(partner_around + swap_vel_around + across + over)
    for q in range(nx):
        leave(swap_rows[q])

    @pl.when(has_near)
    def _():
        leave([seam_near, edge_vel, edge_stress] + near_ends + near_rows)
        leave(seam_ahead_around + ahead_around + edge_vel_around)

    @pl.when(has_far)
    def _():
        leave([seam_pass] + pass_ends + pass_rows + seam_beyond_around + beyond_around)

    @pl.when(pair_lo)
    def _():
        leave(down)

    @pl.when(pair_hi)
    def _():
        leave(up)


def hand_over(flux_in, coef_in, flux_out, coef_out, flux_buf, coef_buf, sems):
    count = flux_in.shape[0]
    pieces = [(flux_in.at[a], flux_buf.at[a], flux_out.at[a]) for a in range(count)]
    pieces.append((coef_in, coef_buf, coef_out))
    take = [pltpu.make_async_copy(a, b, sems.at[0, at]) for at, (a, b, _) in enumerate(pieces)]
    give = [pltpu.make_async_copy(b, c, sems.at[1, at]) for at, (_, b, c) in enumerate(pieces)]
    for c in take:
        c.start()
    for arrive, leave in zip(take, give):
        arrive.wait()
        leave.start()
    for c in give:
        c.wait()


def shards(n_ax, n_az, density, velocity):
    nx, nt, radial = density.shape
    assert radial == 2 * LANES and 2 * 4 * nx * SEAM == LANES and n_ax % 2 == 0
    pr, seam_rows = 2 * nx, nt // 2 + 2 * SUB
    halves, seam = geometry(radial, nt * n_az)

    def field(*lead):
        return pltpu.VMEM(lead + (nt + 2 * EDGE, LANES), jnp.float32)

    def vmem(*shape):
        return pltpu.VMEM(shape, jnp.float32)

    dma = pltpu.SemaphoreType.DMA
    flux, coef = pl.pallas_call(
        functools.partial(kernel, n_ax, n_az, nx, nt),
        out_shape=(
            jax.ShapeDtypeStruct(velocity.shape, jnp.float32),
            jax.ShapeDtypeStruct((nx, radial), jnp.float32),
        ),
        in_specs=[
            pl.BlockSpec(memory_space=pl.ANY),
            pl.BlockSpec(memory_space=pl.ANY),
            pl.BlockSpec(memory_space=pltpu.VMEM),
            pl.BlockSpec(memory_space=pltpu.VMEM),
        ],
        out_specs=(
            pl.BlockSpec(memory_space=pltpu.VMEM),
            pl.BlockSpec(memory_space=pltpu.VMEM),
        ),
        scratch_shapes=[
            field(4, pr + 4),
            field(4, nx + 2),
            field(2, 6, pr + 2),
            field(4, pr + 2),
            field(3, pr + 2),
            field(4, pr + 2),
            field(6, pr),
            field(6, pr),
            vmem(4, seam_rows, LANES),
            field(4),
            field(6),
            field(4),
            field(6),
            field(16),
            field(3),
            vmem(pr, 2, LANES),
            vmem(2, n_az, pr, 2, LANES),
            vmem(2, n_az, 2, LANES),
            vmem(nx + 2, 2, SUB, LANES),
            dma((4,)),
            dma((COPIES,)),
            dma((COPIES,)),
            dma((6 * n_az,)),
            dma((6 * n_az,)),
        ],
        compiler_params=pltpu.CompilerParams(collective_id=0, has_side_effects=True),
        name="closure",
    )(density, velocity, jnp.asarray(halves), jnp.asarray(seam))
    anywhere = pl.BlockSpec(memory_space=pl.ANY)
    return pl.pallas_call(
        hand_over,
        out_shape=(
            jax.ShapeDtypeStruct(flux.shape, jnp.float32),
            jax.ShapeDtypeStruct(coef.shape, jnp.float32),
        ),
        in_specs=[anywhere, anywhere],
        out_specs=(anywhere, anywhere),
        scratch_shapes=[
            pltpu.VMEM(flux.shape, jnp.float32),
            pltpu.VMEM(coef.shape, jnp.float32),
            dma((2, flux.shape[0] + 1)),
        ],
        name="hand_over",
    )(flux, coef)


def solution(mesh):
    in_specs = (P("ax", "az", None), P(None, "ax", "az", None))
    out_specs = (P(None, "ax", "az", None), P("ax", None))
    body = functools.partial(shards, mesh.shape["ax"], mesh.shape["az"])
    return jax.shard_map(body, mesh=mesh, in_specs=in_specs, out_specs=out_specs, check_vma=False)
```

time: 38.2 us -> 37.1 us (0.971)
  Pallas kernels: 37.3 us -> 36.3 us
    pallas_call x1, Pallas kernels: 35.4 us -> 34.4 us  [shards(): pl.pallas_call(functools.partial(kernel, n_ax, n_az, nx, nt), out_shape=(...]
where the time goes in v1:
time: 37.1 us; the launch traced here: 36.9 us
  Pallas kernels  36.3 us (98%)
  between operations  0.64 us (2%)
    pallas_call x1, Pallas kernels, shards(): pl.pallas_call(functools.partial(kernel, n_ax, n_az, nx, nt), out_shape=(...  34.4 us
    pallas_call x1, Pallas kernels, shards(): pl.pallas_call(hand_over, out_shape=(jax.ShapeDtypeStruct(flux.shape, jnp...  1.9 us

profile of v1, /device:TPU:0, one launch (start us, length us, event | category | flops | bytes accessed | tf_op | source)
XLA Modules:
  0.0 36.9 jit_solution(1009700408100921042)
XLA Ops:
  0.6 34.4 %closure.1 = (f32[3,4,64,256]{3,2,1,0:T(8,128)}, f32[4,256]{1,0:T(4,128)}) custom-call(f32[4,64,256]{2,1,0:T(8,128)} %rho_ref.1, f32[3,4,64,256]{3,2,1,0:T(8,128)} %vel_ref.1, f32[8,2,8,128]{3,2,1,0:T(8,128)} %constant.4.clone.geo_ref, f32[4,8,128]{2,1,0:T(8,128)} %constant.5.clone.seam_ref), custom_call_target="tpu_custom_call" | custom-call | tf_op jit(solution)/shard_map/closure/pallas_call | solution.py:762
  35.0 1.9 %hand_over.1 = (f32[3,4,64,256]{3,2,1,0:T(8,128)}, f32[4,256]{1,0:T(4,128)}) custom-call(f32[3,4,64,256]{3,2,1,0:T(8,128)} %get-tuple-element.4.flux_in, f32[4,256]{1,0:T(4,128)} %get-tuple-element.5.coef_in), custom_call_target="tpu_custom_call" | custom-call | tf_op jit(solution)/shard_map/hand_over/pallas_call | solution.py:808

commit v2 on v1

--- a/solution.py
+++ b/solution.py
@@ -23,6 +23,7 @@
 EDGE = 16
 SEAM = 4
 COPIES = 64
+BLOCKS = {'first': 16, 'hat': 16, 'model': 16, 'closure': 16, 'other': 16, 'flux': 16, 'seam': 16}
 MESH_ID = pl.DeviceIdType.MESH
 
 
@@ -100,9 +101,9 @@
 
 def kernel(
     n_ax, n_az, nx, nt,
-    rho_ref, vel_ref, geo_ref, seam_ref, flux_ref, coef_ref,
+    rho_ref, vel_ref, geo_in, seam_in, flux_ref, coef_ref,
     S, T, M, H, V, HM, PX, MX, E, G, GM, GH, GP, GX, GV,
-    part, rec, rec_out, CS, own_sem, send_sem, recv_sem, sum_send, sum_recv,
+    part, rec, rec_out, CS, geo_ref, seam_ref, own_sem, send_sem, recv_sem, sum_send, sum_recv,
 ):
     pr = 2 * nx
     me_ax, me_az = lax.axis_index("ax"), lax.axis_index("az")
@@ -143,7 +144,11 @@
         pltpu.make_async_copy(
             vel_ref.at[:, :, :, lanes_other], T.at[pl.ds(1, 3), pl.ds(1, nx), cols, :], own_sem.at[3]),
     ]
-    for c in own:
+    tables = [
+        pltpu.make_async_copy(geo_in, geo_ref, own_sem.at[4]),
+        pltpu.make_async_copy(seam_in, seam_ref, own_sem.at[5]),
+    ]
+    for c in own + tables:
         c.start()
 
     barrier = pltpu.get_barrier_semaphore()
@@ -298,7 +303,8 @@
                 packed = jnp.where((half >= first) & (half < first + SEAM), high, packed)
         E[s_own, pl.ds(SUB, fold), :] = packed
 
-    seam_lane = lanes_at(wide)
+    n_seam = math.gcd(BLOCKS["seam"], wide)
+    seam_lane = lanes_at(n_seam)
     seam_row = seam_lane // SEAM
     at_bottom = seam_row == jnp.where(pair_lo, -1, nx)
     at_top = seam_row == jnp.where(pair_hi, -1, nx + pr - 1)
@@ -315,12 +321,9 @@
     def seam_rise(x):
         return pltpu.roll(x, LANES - 1, 1) - pltpu.roll(x, 1, 1)
 
-    span = pl.ds(outer_cols, wide)
-    span_before, span_after = pl.ds(outer_cols - 1, wide), pl.ds(outer_cols + 1, wide)
-
-    def seam_turn(ref, a):
-        x = ref[a, span, :]
-        return (ref[a, span_before, :] + ref[a, span_after, :]) + (x + x)
+    def seam_turn(ref, a, c, n):
+        x = ref[a, pl.ds(c, n), :]
+        return (ref[a, pl.ds(c - 1, n), :] + ref[a, pl.ds(c + 1, n), :]) + (x + x)
 
     def seam_pass_all():
         lane = lanes_at(fold + SUB)
@@ -338,33 +341,38 @@
             G[a, pl.ds(EDGE, fold), :] = low[:fold]
             G[a, pl.ds(EDGE + fold, fold), :] = high[SUB:]
             G[a, pl.ds(EDGE + nt, SUB), :] = low[fold:]
-        rho = G[0, span, :]
-        vel = [G[1 + a, span, :] for a in range(3)]
-        inv_r, az_scale, width = (spread(seam_ref[g], wide) for g in (0, 1, 2))
-        dx = [seam_above(v) - seam_below(v) for v in vel]
-        dr = [seam_rise(v) * (0.5 / STEP_RADIAL) for v in vel]
-        dt = [(G[1 + a, span_after, :] - G[1 + a, span_before, :]) * az_scale for a in range(3)]
-        dev, size = strain(dx, dr, dt, vel[1], vel[2], inv_r)
-        scale = rho * width * size
-        for a in range(6):
-            GM[a, span, :] = seam_axial(scale * dev[a])
-        mom = [rho * v for v in vel]
-        GH[0, span, :] = seam_axial(rho)
-        for a in range(3):
-            GH[1 + a, span, :] = seam_axial(mom[a])
-        for at, (a, b) in enumerate(PAIRS):
-            GP[at, span, :] = seam_axial(mom[a] * vel[b])
-        hat = []
-        for a in range(4):
-            s = seam_turn(GH, a)
-            GX[a, span, :] = s
-            hat.append(((pltpu.roll(s, 1, 1) + pltpu.roll(s, LANES - 1, 1)) + (s + s)) * (1.0 / 64.0))
-        inv = 1.0 / hat[0]
-        for a in range(3):
-            GV[a, span, :] = hat[1 + a] * inv
-        for a in range(6):
-            GX[4 + a, span, :] = seam_turn(GP, a)
-            GX[10 + a, span, :] = seam_turn(GM, a)
+        parts = [(c, n_seam) for c in range(outer_cols, outer_cols + wide, n_seam)]
+        for c, n in parts:
+            at, at_before, at_after = pl.ds(c, n), pl.ds(c - 1, n), pl.ds(c + 1, n)
+            rho = G[0, at, :]
+            vel = [G[1 + a, at, :] for a in range(3)]
+            inv_r, az_scale, width = (spread(seam_ref[g], n) for g in (0, 1, 2))
+            dx = [seam_above(v) - seam_below(v) for v in vel]
+            dr = [seam_rise(v) * (0.5 / STEP_RADIAL) for v in vel]
+            dt = [(G[1 + a, at_after, :] - G[1 + a, at_before, :]) * az_scale for a in range(3)]
+            dev, size = strain(dx, dr, dt, vel[1], vel[2], inv_r)
+            scale = rho * width * size
+            for a in range(6):
+                GM[a, at, :] = seam_axial(scale * dev[a])
+            mom = [rho * v for v in vel]
+            GH[0, at, :] = seam_axial(rho)
+            for a in range(3):
+                GH[1 + a, at, :] = seam_axial(mom[a])
+            for q, (a, b) in enumerate(PAIRS):
+                GP[q, at, :] = seam_axial(mom[a] * vel[b])
+        for c, n in parts:
+            at = pl.ds(c, n)
+            hat = []
+            for a in range(4):
+                s = seam_turn(GH, a, c, n)
+                GX[a, at, :] = s
+                hat.append(((pltpu.roll(s, 1, 1) + pltpu.roll(s, LANES - 1, 1)) + (s + s)) * (1.0 / 64.0))
+            inv = 1.0 / hat[0]
+            for a in range(3):
+                GV[a, at, :] = hat[1 + a] * inv
+            for a in range(6):
+                GX[4 + a, at, :] = seam_turn(GP, a, c, n)
+                GX[10 + a, at, :] = seam_turn(GM, a, c, n)
 
     end_lane = pick(LANES - 1, 0)
 
@@ -401,62 +409,70 @@
         return ref[a, row, pl.ds(first + 1, n), :] - ref[a, row, pl.ds(first - 1, n), :]
 
     def first_pass(r, with_pairs):
-        n, c = wide, outer_cols
-        rows = (low(r) + 2, r + 2, high(r) + 2)
-        rho = [S[0, q, pl.ds(c, n), :] for q in rows]
-        vel = [[S[1 + a, q, pl.ds(c, n), :] for a in range(3)] for q in rows]
-        inv_r, az_scale, width = (spread(geo_ref[g, mine], n) for g in (0, 1, 2))
-        dx = [vel[2][a] - vel[0][a] for a in range(3)]
-        dr = [seam_slope(vel[1][a], G, 1 + a, c, r) * (0.5 / STEP_RADIAL) for a in range(3)]
-        dt = [turn_slope(S, 1 + a, r + 2, c, n) * az_scale for a in range(3)]
-        dev, size = strain(dx, dr, dt, vel[1][1], vel[1][2], inv_r)
-        scale = rho[1] * width * size
-        for a in range(6):
-            M[mine, a, r + 1, pl.ds(c, n), :] = scale * dev[a]
-        mom = [[rho[q] * vel[q][a] for a in range(3)] for q in range(3)]
-        H[0, r + 1, pl.ds(c, n), :] = (rho[0] + rho[1]) + (rho[1] + rho[2])
-        for a in range(3):
-            H[1 + a, r + 1, pl.ds(c, n), :] = (mom[0][a] + mom[1][a]) + (mom[1][a] + mom[2][a])
-        if with_pairs:
+        n = math.gcd(BLOCKS["first"], wide)
+        for c in range(outer_cols, outer_cols + wide, n):
+            rows = (low(r) + 2, r + 2, high(r) + 2)
+            rho = [S[0, q, pl.ds(c, n), :] for q in rows]
+            vel = [[S[1 + a, q, pl.ds(c, n), :] for a in range(3)] for q in rows]
+            inv_r, az_scale, width = (spread(geo_ref[g, mine], n) for g in (0, 1, 2))
+            dx = [vel[2][a] - vel[0][a] for a in range(3)]
+            dr = [seam_slope(vel[1][a], G, 1 + a, c, r) * (0.5 / STEP_RADIAL) for a in range(3)]
+            dt = [turn_slope(S, 1 + a, r + 2, c, n) * az_scale for a in range(3)]
+            dev, size = strain(dx, dr, dt, vel[1][1], vel[1][2], inv_r)
+            scale = rho[1] * width * size
+            for a in range(6):
+                M[mine, a, r + 1, pl.ds(c, n), :] = scale * dev[a]
+            mom = [[rho[q] * vel[q][a] for a in range(3)] for q in range(3)]
+            H[0, r + 1, pl.ds(c, n), :] = (rho[0] + rho[1]) + (rho[1] + rho[2])
+            for a in range(3):
+                H[1 + a, r + 1, pl.ds(c, n), :] = (mom[0][a] + mom[1][a]) + (mom[1][a] + mom[2][a])
+            if with_pairs:
+                for at, (a, b) in enumerate(PAIRS):
+                    p = [mom[q][a] * vel[q][b] for q in range(3)]
+                    PX[at, r, pl.ds(c, n), :] = (p[0] + p[1]) + (p[1] + p[2])
+
+    def hat_pass(r):
+        n = math.gcd(BLOCKS["hat"], wide)
+        for c in range(outer_cols, outer_cols + wide, n):
+            hat = [smooth(H, a, r + 1, c, n, a, r) for a in range(4)]
+            inv = 1.0 / hat[0]
+            for a in range(4):
+                HM[a, r + 1, pl.ds(c, n), :] = hat[a]
+            for a in range(3):
+                V[a, r + 1, pl.ds(c, n), :] = hat[1 + a] * inv
+
+    def model_pass(r):
+        n = math.gcd(BLOCKS["model"], wide)
+        for c in range(outer_cols, outer_cols + wide, n):
+            for a in range(6):
+                x = M[mine, a, r + 1, pl.ds(c, n), :]
+                lo = M[mine, a, low(r) + 1, pl.ds(c, n), :]
+                MX[a, r, pl.ds(c, n), :] = (lo + x) + (x + M[mine, a, high(r) + 1, pl.ds(c, n), :])
+
+    def closure_pass(r):
+        sums = [0.0, 0.0]
+        n = math.gcd(BLOCKS["closure"], nt)
+        for c in range(EDGE, EDGE + nt, n):
+            inv_r, az_scale, width4 = (spread(geo_ref[g, mine], n) for g in (0, 1, 3))
+            hv = [V[a, r + 1, pl.ds(c, n), :] for a in range(3)]
+            hm = [HM[1 + a, r + 1, pl.ds(c, n), :] for a in range(3)]
+            dx = [V[a, high(r) + 1, pl.ds(c, n), :] - V[a, low(r) + 1, pl.ds(c, n), :] for a in range(3)]
+            dr = [seam_slope(hv[a], GV, a, c, r) * (0.5 / STEP_RADIAL) for a in range(3)]
+            dt = [turn_slope(V, a, r + 1, c, n) * az_scale for a in range(3)]
+            dev, size = strain(dx, dr, dt, hv[1], hv[2], inv_r)
+            scale = width4 * HM[0, r + 1, pl.ds(c, n), :] * size
+            lm, mm = [], []
             for at, (a, b) in enumerate(PAIRS):
-                p = [mom[q][a] * vel[q][b] for q in range(3)]
-                PX[at, r, pl.ds(c, n), :] = (p[0] + p[1]) + (p[1] + p[2])
-
-    def hat_pass(r):
-        n, c = wide, outer_cols
-        hat = [smooth(H, a, r + 1, c, n, a, r) for a in range(4)]
-        inv = 1.0 / hat[0]
-        for a in range(4):
-            HM[a, r + 1, pl.ds(c, n), :] = hat[a]
-        for a in range(3):
-            V[a, r + 1, pl.ds(c, n), :] = hat[1 + a] * inv
-
-    def model_pass(r):
-        n, c = wide, outer_cols
-        for a in range(6):
-            x = M[mine, a, r + 1, pl.ds(c, n), :]
-            lo = M[mine, a, low(r) + 1, pl.ds(c, n), :]
-            MX[a, r, pl.ds(c, n), :] = (lo + x) + (x + M[mine, a, high(r) + 1, pl.ds(c, n), :])
-
-    def closure_pass(r):
-        n, c = nt, EDGE
-        inv_r, az_scale, width4 = (spread(geo_ref[g, mine], n) for g in (0, 1, 3))
-        hv = [V[a, r + 1, pl.ds(c, n), :] for a in range(3)]
-        hm = [HM[1 + a, r + 1, pl.ds(c, n), :] for a in range(3)]
-        dx = [V[a, high(r) + 1, pl.ds(c, n), :] - V[a, low(r) + 1, pl.ds(c, n), :] for a in range(3)]
-        dr = [seam_slope(hv[a], GV, a, c, r) * (0.5 / STEP_RADIAL) for a in range(3)]
-        dt = [turn_slope(V, a, r + 1, c, n) * az_scale for a in range(3)]
-        dev, size = strain(dx, dr, dt, hv[1], hv[2], inv_r)
-        scale = width4 * HM[0, r + 1, pl.ds(c, n), :] * size
-        lm, mm = [], []
-        for at, (a, b) in enumerate(PAIRS):
-            mixed = scale * dev[at] - smooth(MX, at, r, c, n, 10 + at, r)
-            leonard = smooth(PX, at, r, c, n, 4 + at, r) - hm[a] * hv[b]
-            lm.append(leonard * mixed)
-            mm.append(mixed * mixed)
-        for q, terms in enumerate((lm, mm)):
-            diagonal, cross = (sum(terms[a] for a in group) for group in (DIAGONAL, CROSS))
-            part[r, pl.ds(q, 1), :] = jnp.sum(diagonal + 2.0 * cross, axis=0, keepdims=True)
+                mixed = scale * dev[at] - smooth(MX, at, r, c, n, 10 + at, r)
+                leonard = smooth(PX, at, r, c, n, 4 + at, r) - hm[a] * hv[b]
+                lm.append(leonard * mixed)
+                mm.append(mixed * mixed)
+            for q, terms in enumerate((lm, mm)):
+                diagonal, cross = (sum(terms[a] for a in group) for group in (DIAGONAL, CROSS))
+                cells = diagonal + 2.0 * cross
+                sums[q] += sum(cells[at:at + SUB] for at in range(0, n, SUB))
+        for q in range(2):
+            part[r, pl.ds(q, 1), :] = jnp.sum(sums[q], axis=0, keepdims=True)
 
     def first_two(first, count, with_pairs=True):
         sweep(first, count, lambda r: first_pass(r, with_pairs))
@@ -469,22 +485,23 @@
     seam_far = pick(LANES - 1, 1)
 
     def other_half(i):
-        n, c = wide, outer_cols
-        inv_r, az_scale, width = (spread(geo_ref[g, other], n) for g in (0, 1, 2))
-        lo = jnp.maximum(i - 1, jnp.where(has_lo, -1, 0)) + 1
-        hi = jnp.minimum(i + 1, jnp.where(has_hi, nx, nx - 1)) + 1
-        vel = [T[1 + a, i + 1, pl.ds(c, n), :] for a in range(3)]
-        dx = [T[1 + a, hi, pl.ds(c, n), :] - T[1 + a, lo, pl.ds(c, n), :] for a in range(3)]
-        dr = []
-        for a in range(3):
-            far = pltpu.roll(S[1 + a, own_at + i, pl.ds(c, n), :], pick(1, LANES - 1), 1)
-            before_, after_ = sides(vel[a], jnp.where(lane_of(far) == pick(0, LANES - 1), far, vel[a]))
-            dr.append((after_ - before_) * (0.5 / STEP_RADIAL))
-        dt = [turn_slope(T, 1 + a, i + 1, c, n) * az_scale for a in range(3)]
-        dev, size = strain(dx, dr, dt, vel[1], vel[2], inv_r)
-        scale = T[0, i + 1, pl.ds(c, n), :] * width * size
-        for a in range(6):
-            M[other, a, own_row + i + 1, pl.ds(c, n), :] = scale * dev[a]
+        n = math.gcd(BLOCKS["other"], wide)
+        for c in range(outer_cols, outer_cols + wide, n):
+            inv_r, az_scale, width = (spread(geo_ref[g, other], n) for g in (0, 1, 2))
+            lo = jnp.maximum(i - 1, jnp.where(has_lo, -1, 0)) + 1
+            hi = jnp.minimum(i + 1, jnp.where(has_hi, nx, nx - 1)) + 1
+            vel = [T[1 + a, i + 1, pl.ds(c, n), :] for a in range(3)]
+            dx = [T[1 + a, hi, pl.ds(c, n), :] - T[1 + a, lo, pl.ds(c, n), :] for a in range(3)]
+            dr = []
+            for a in range(3):
+                far = pltpu.roll(S[1 + a, own_at + i, pl.ds(c, n), :], pick(1, LANES - 1), 1)
+                before_, after_ = sides(vel[a], jnp.where(lane_of(far) == pick(0, LANES - 1), far, vel[a]))
+                dr.append((after_ - before_) * (0.5 / STEP_RADIAL))
+            dt = [turn_slope(T, 1 + a, i + 1, c, n) * az_scale for a in range(3)]
+            dev, size = strain(dx, dr, dt, vel[1], vel[2], inv_r)
+            scale = T[0, i + 1, pl.ds(c, n), :] * width * size
+            for a in range(6):
+                M[other, a, own_row + i + 1, pl.ds(c, n), :] = scale * dev[a]
 
     def rows_of(first, count, body):
         def step(at, carry):
@@ -518,6 +535,8 @@
         start(seam_beyond_around)
 
     arrive(own_around)
+    for c in tables:
+        c.wait()
     rows_of(1, nx - 2, other_half)
 
     @pl.when(has_near)
@@ -661,35 +680,36 @@
             coef_ref[pl.ds(i, 1), pl.ds(h * LANES, LANES)] = -0.5 * CS[i + 1, h, pl.ds(0, 1), :]
 
     def flux_pass(i):
-        n, c = nt, EDGE
-        r = own_row + i + 1
-        inv_r, az_scale, radius, back, radius2, back2 = (spread(geo_ref[g], n) for g in (0, 1, 4, 5, 6, 7))
-        lo = jnp.maximum(i - 1, jnp.where(has_lo, -1, 0)) + 1
-        hi = jnp.minimum(i + 1, jnp.where(has_hi, nx, nx - 1)) + 1
-        here, below, above = (spread(CS[q], n) for q in (i + 1, lo, hi))
-
-        def at(a, row, shift=0):
-            return M[:, a, row, pl.ds(c + shift, n), :]
-
-        def axial(a):
-            return above * at(a, own_row + hi) - below * at(a, own_row + lo)
-
-        def around_of(a):
-            return (at(a, r, 1) - at(a, r, -1)) * turn
-
-        turn = here * az_scale
-        once = here * radius
-        d_xr = rise(once * at(1, r)) * back
-        d_rr = rise(once * at(3, r)) * back
-        d_rt = rise(here * radius2 * at(5, r)) * back2
-        out = (
-            axial(0) + d_xr + around_of(2),
-            axial(1) + d_rr + around_of(5) - here * at(4, r) * inv_r,
-            axial(2) + d_rt + around_of(4),
-        )
-        for a in range(3):
-            for h in range(2):
-                flux_ref[a, i, :, pl.ds(h * LANES, LANES)] = out[a][h]
+        n = math.gcd(BLOCKS["flux"], nt)
+        for c in range(EDGE, EDGE + nt, n):
+            r = own_row + i + 1
+            inv_r, az_scale, radius, back, radius2, back2 = (spread(geo_ref[g], n) for g in (0, 1, 4, 5, 6, 7))
+            lo = jnp.maximum(i - 1, jnp.where(has_lo, -1, 0)) + 1
+            hi = jnp.minimum(i + 1, jnp.where(has_hi, nx, nx - 1)) + 1
+            here, below, above = (spread(CS[q], n) for q in (i + 1, lo, hi))
+
+            def at(a, row, shift=0):
+                return M[:, a, row, pl.ds(c + shift, n), :]
+
+            def axial(a):
+                return above * at(a, own_row + hi) - below * at(a, own_row + lo)
+
+            def around_of(a):
+                return (at(a, r, 1) - at(a, r, -1)) * turn
+
+            turn = here * az_scale
+            once = here * radius
+            d_xr = rise(once * at(1, r)) * back
+            d_rr = rise(once * at(3, r)) * back
+            d_rt = rise(here * radius2 * at(5, r)) * back2
+            out = (
+                axial(0) + d_xr + around_of(2),
+                axial(1) + d_rr + around_of(5) - here * at(4, r) * inv_r,
+                axial(2) + d_rt + around_of(4),
+            )
+            for a in range(3):
+                for h in range(2):
+                    flux_ref[a, i, pl.ds(c - EDGE, n), pl.ds(h * LANES, LANES)] = out[a][h]
 
     rows_of(1, nx - 2, flux_pass)
 
@@ -735,13 +755,9 @@
     count = flux_in.shape[0]
     pieces = [(flux_in.at[a], flux_buf.at[a], flux_out.at[a]) for a in range(count)]
     pieces.append((coef_in, coef_buf, coef_out))
-    take = [pltpu.make_async_copy(a, b, sems.at[0, at]) for at, (a, b, _) in enumerate(pieces)]
-    give = [pltpu.make_async_copy(b, c, sems.at[1, at]) for at, (_, b, c) in enumerate(pieces)]
-    for c in take:
+    give = [pltpu.make_async_copy(a, c, sems.at[1, at]) for at, (a, b, c) in enumerate(pieces)]
+    for c in give:
         c.start()
-    for arrive, leave in zip(take, give):
-        arrive.wait()
-        leave.start()
     for c in give:
         c.wait()
 
@@ -766,10 +782,10 @@
             jax.ShapeDtypeStruct((nx, radial), jnp.float32),
         ),
         in_specs=[
-            pl.BlockSpec(memory_space=pl.ANY),
-            pl.BlockSpec(memory_space=pl.ANY),
-            pl.BlockSpec(memory_space=pltpu.VMEM),
-            pl.BlockSpec(memory_space=pltpu.VMEM),
+            pl.BlockSpec(memory_space=pltpu.HBM),
+            pl.BlockSpec(memory_space=pltpu.HBM),
+            pl.BlockSpec(memory_space=pltpu.HBM),
+            pl.BlockSpec(memory_space=pltpu.HBM),
         ],
         out_specs=(
             pl.BlockSpec(memory_space=pltpu.VMEM),
@@ -795,15 +811,18 @@
             vmem(2, n_az, pr, 2, LANES),
             vmem(2, n_az, 2, LANES),
             vmem(nx + 2, 2, SUB, LANES),
-            dma((4,)),
+            vmem(*halves.shape),
+            vmem(*seam.shape),
+            dma((6,)),
             dma((COPIES,)),
             dma((COPIES,)),
             dma((6 * n_az,)),
             dma((6 * n_az,)),
         ],
-        compiler_params=pltpu.CompilerParams(collective_id=0, has_side_effects=True),
+        compiler_params=pltpu.CompilerParams(collective_id=0, has_side_effects=True, vmem_limit_bytes=40 << 20),
         name="closure",
-    )(density, velocity, jnp.asarray(halves), jnp.asarray(seam))
+    )(pltpu.with_memory_space_constraint(density, pltpu.HBM), pltpu.with_memory_space_constraint(velocity, pltpu.HBM), pltpu.with_memory_space_constraint(jnp.asarray(halves), pltpu.HBM), pltpu.with_memory_space_constraint(jnp.asarray(seam), pltpu.HBM))
+    flux, coef = (pltpu.with_memory_space_constraint(x, pltpu.VMEM) for x in (flux, coef))
     anywhere = pl.BlockSpec(memory_space=pl.ANY)
     return pl.pallas_call(
         hand_over,
@@ -811,8 +830,8 @@
             jax.ShapeDtypeStruct(flux.shape, jnp.float32),
             jax.ShapeDtypeStruct(coef.shape, jnp.float32),
         ),
-        in_specs=[anywhere, anywhere],
-        out_specs=(anywhere, anywhere),
+        in_specs=[pl.BlockSpec(memory_space=pltpu.VMEM)] * 2,
+        out_specs=(pl.BlockSpec(memory_space=pltpu.HBM),) * 2,
         scratch_shapes=[
             pltpu.VMEM(flux.shape, jnp.float32),
             pltpu.VMEM(coef.shape, jnp.float32),

time: 37.1 us -> 33.9 us (0.914)
  Pallas kernels: 36.3 us -> 33.2 us
    pallas_call x1, Pallas kernels: 34.4 us -> 32.2 us  [shards(): pl.pallas_call(functools.partial(kernel, n_ax, n_az, nx, nt), out_shape=(...]
    pallas_call x1, Pallas kernels: 1.9 us -> 0.95 us  [shards(): pl.pallas_call(hand_over, out_shape=(jax.ShapeDtypeStruct(flux.shape, jnp...]
where the time goes in v2:
time: 33.9 us; the launch traced here: 33.8 us
  Pallas kernels  33.2 us (98%)
  between operations  0.64 us (2%)
    pallas_call x1, Pallas kernels, shards(): pl.pallas_call(functools.partial(kernel, n_ax, n_az, nx, nt), out_shape=(...  32.2 us
    pallas_call x1, Pallas kernels, shards(): pl.pallas_call(hand_over, out_shape=(jax.ShapeDtypeStruct(flux.shape, jnp...  0.95 us

profile of v2, /device:TPU:0, one launch (start us, length us, event | category | flops | bytes accessed | tf_op | source)
XLA Modules:
  0.0 33.8 jit_solution(16396322674515771925)
XLA Ops:
  0.6 32.2 %closure.1 = (f32[3,4,64,256]{3,2,1,0:T(8,128)S(1)}, f32[4,256]{1,0:T(4,128)S(1)}) custom-call(f32[4,64,256]{2,1,0:T(8,128)} %rho_ref.1, f32[3,4,64,256]{3,2,1,0:T(8,128)} %vel_ref.1, f32[8,2,8,128]{3,2,1,0:T(8,128)} %constant.4.clone.geo_in, f32[4,8,128]{2,1,0:T(8,128)} %constant.5.clone.seam_in), custom_call_target="tpu_custom_call" | custom-call | tf_op jit(solution)/shard_map/closure/pallas_call | solution.py:778
  32.8 1.0 %hand_over.1 = (f32[3,4,64,256]{3,2,1,0:T(8,128)}, f32[4,256]{1,0:T(4,128)}) custom-call(f32[3,4,64,256]{3,2,1,0:T(8,128)S(1)} %get-tuple-element.4.flux_in, f32[4,256]{1,0:T(4,128)S(1)} %get-tuple-element.5.coef_in), custom_call_target="tpu_custom_call" | custom-call | tf_op jit(solution)/shard_map/hand_over/pallas_call | solution.py:827

commit v3 on v2

--- a/solution.py
+++ b/solution.py
@@ -15,13 +15,12 @@
 INNER_RADIUS = 10.0
 FILTER_RATIO = 2.0
 TINY = 1e-06
-PAIRS = ((0, 0), (0, 1), (0, 2), (1, 1), (2, 2), (1, 2))
-DIAGONAL = (0, 3, 4)
-CROSS = (1, 2, 5)
+KEPT = (0, 3, 1, 2, 5)
+CROSS = ((0, 1), (0, 2), (1, 2))
 LANES = 128
 SUB = 8
 EDGE = 16
-SEAM = 4
+SEAM = 8
 COPIES = 64
 BLOCKS = {'first': 16, 'hat': 16, 'model': 16, 'closure': 16, 'other': 16, 'flux': 16, 'seam': 16}
 MESH_ID = pl.DeviceIdType.MESH
@@ -72,12 +71,44 @@
     return after(x) - before(x)
 
 
-def sides(x, end):
+def sides(x):
     lane = lane_of(x)
     return (
-        jnp.where(lane == 0, end, pltpu.roll(x, 1, 1)),
-        jnp.where(lane == LANES - 1, end, pltpu.roll(x, LANES - 1, 1)),
+        jnp.where(lane == 0, x, pltpu.roll(x, 1, 1)),
+        jnp.where(lane == LANES - 1, x, pltpu.roll(x, LANES - 1, 1)),
     )
+
+
+def radial(s):
+    lo, hi = sides(s)
+    return ((lo + hi) + (s + s)) * (1.0 / 64.0)
+
+
+def slope(x):
+    lo, hi = sides(x)
+    return (hi - lo) * (0.5 / STEP_RADIAL)
+
+
+def pairs(mom, vel):
+    azimuthal = mom[2] * vel[2]
+    return [mom[a] * vel[a] - azimuthal for a in (0, 1)] + [mom[a] * vel[b] for a, b in CROSS]
+
+
+def contractions(dev, scale, hat_pairs, hat_model, hat_mom, hat_vel):
+    mixed = [scale * dev[a] - m for a, m in zip(KEPT, hat_model)]
+    leonard = [p - q for p, q in zip(hat_pairs, pairs(hat_mom, hat_vel))]
+
+    def cross(left, right):
+        return 2.0 * (left[2] * right[2] + left[3] * right[3] + left[4] * right[4])
+
+    azimuthal = mixed[0] + mixed[1]
+    lm = leonard[0] * mixed[0] + leonard[1] * mixed[1] + cross(leonard, mixed)
+    mm = mixed[0] * mixed[0] + mixed[1] * mixed[1] + azimuthal * azimuthal + cross(mixed, mixed)
+    return lm, mm
+
+
+def fold_rows(cells):
+    return sum(cells[at:at + SUB] for at in range(0, cells.shape[0], SUB))
 
 
 def strain(dx, dr, dt, ur, ut, inv_r):
@@ -102,7 +133,7 @@
 def kernel(
     n_ax, n_az, nx, nt,
     rho_ref, vel_ref, geo_in, seam_in, flux_ref, coef_ref,
-    S, T, M, H, V, HM, PX, MX, E, G, GM, GH, GP, GX, GV,
+    S, T, M, H, V, HM, PX, MX, E, G, GM, GH, GP, GHM, GV, SP,
     part, rec, rec_out, CS, geo_ref, seam_ref, own_sem, send_sem, recv_sem, sum_send, sum_recv,
 ):
     pr = 2 * nx
@@ -156,18 +187,23 @@
     def greet(ax, az):
         pl.semaphore_signal(barrier, inc=1, device_id=(ax, az), device_id_type=MESH_ID)
 
-    for d in range(1, n_az):
+    short = n_az == 4
+    for d in (1, n_az - 1) if short else range(1, n_az):
         greet(me_ax, lax.rem(me_az + d, n_az))
-    peers = n_az - 1
-    for step in (-1, 1, -2, 2):
+    peers = 2 if short else n_az - 1
+    if short:
+        greet(partner, me_az)
+        peers = peers + 1
+    for step in (-2, 2) if short else (-1, 1, -2, 2):
         there = (me_ax + step >= 0) & (me_ax + step < n_ax)
+        reach = 1 if short else n_az
 
         @pl.when(there)
         def _():
-            for d in range(n_az):
+            for d in range(reach):
                 greet(me_ax + step, lax.rem(me_az + d, n_az))
 
-        peers = peers + jnp.where(there, n_az, 0)
+        peers = peers + jnp.where(there, reach, 0)
 
     ids = itertools.count()
 
@@ -201,13 +237,12 @@
             remote(ref.at[lead, rows, at[2], :], ref.at[lead, rows, at[3], :], me_ax, left),
         ]
 
-    fold = nt // 2
-    whole = pl.ds(SUB, fold)
+    whole = pl.ds(SUB, nt)
 
     def seam_around(s):
         return [
-            remote(E.at[s, pl.ds(fold, SUB), :], E.at[s, pl.ds(0, SUB), :], me_ax, right),
-            remote(E.at[s, pl.ds(SUB, SUB), :], E.at[s, pl.ds(SUB + fold, SUB), :], me_ax, left),
+            remote(E.at[s, pl.ds(nt, SUB), :], E.at[s, pl.ds(0, SUB), :], me_ax, right),
+            remote(E.at[s, pl.ds(SUB, SUB), :], E.at[s, pl.ds(SUB + nt, SUB), :], me_ax, left),
         ]
 
     s_own, s_partner, s_beyond, s_ahead = 1 + odd, 2 - odd, pick(3, 0), pick(0, 3)
@@ -290,18 +325,14 @@
     def pack_seam():
         lane = lanes_at(nt)
         from_mine = jnp.where(lane >= LANES - SEAM // 2, 1, 0) == even
-        half = lanes_at(fold)
-        packed = jnp.zeros((fold, LANES), jnp.float32)
+        packed = jnp.zeros((nt, LANES), jnp.float32)
         for a in range(4):
             for i in range(nx):
                 first = (a * nx + i) * SEAM
                 x = jnp.where(from_mine, S[a, own_at + i, pl.ds(EDGE, nt), :], T[a, 1 + i, pl.ds(EDGE, nt), :])
-                low = pltpu.roll(x[:fold], (first + SEAM // 2) % LANES, 1)
-                high = pltpu.roll(x[fold:], (first + SEAM // 2 + LANES // 2) % LANES, 1)
-                packed = jnp.where((half >= first) & (half < first + SEAM), low, packed)
-                first += LANES // 2
-                packed = jnp.where((half >= first) & (half < first + SEAM), high, packed)
-        E[s_own, pl.ds(SUB, fold), :] = packed
+                x = pltpu.roll(x, (first + SEAM // 2) % LANES, 1)
+                packed = jnp.where((lane >= first) & (lane < first + SEAM), x, packed)
+        E[s_own, whole, :] = packed
 
     n_seam = math.gcd(BLOCKS["seam"], wide)
     seam_lane = lanes_at(n_seam)
@@ -318,78 +349,90 @@
     def seam_axial(x):
         return (seam_below(x) + x) + (x + seam_above(x))
 
-    def seam_rise(x):
-        return pltpu.roll(x, LANES - 1, 1) - pltpu.roll(x, 1, 1)
+    def seam_slope(x):
+        return (pltpu.roll(x, LANES - 1, 1) - pltpu.roll(x, 1, 1)) * (0.5 / STEP_RADIAL)
+
+    def seam_radial(s):
+        return ((pltpu.roll(s, 1, 1) + pltpu.roll(s, LANES - 1, 1)) + (s + s)) * (1.0 / 64.0)
 
     def seam_turn(ref, a, c, n):
         x = ref[a, pl.ds(c, n), :]
         return (ref[a, pl.ds(c - 1, n), :] + ref[a, pl.ds(c + 1, n), :]) + (x + x)
 
     def seam_pass_all():
-        lane = lanes_at(fold + SUB)
+        tiles = [(c, n_seam) for c in range(outer_cols, outer_cols + wide, n_seam)]
+        inner = [(c, n_seam) for c in range(EDGE, EDGE + nt, n_seam)]
+        lane = lanes_at(wide)
         per = nx * SEAM
         for a in range(4):
-            low = jnp.zeros((fold + SUB, LANES), jnp.float32)
-            high = low
+            packed = jnp.zeros((wide, LANES), jnp.float32)
             for s in range(4):
-                here = (lane >= s * per) & (lane < (s + 1) * per)
-                x = pltpu.roll(E[s, pl.ds(SUB, fold + SUB), :], (s * per - a * per) % LANES, 1)
-                low = jnp.where(here, x, low)
-                x = pltpu.roll(E[s, pl.ds(0, fold + SUB), :], (s * per - a * per - LANES // 2) % LANES, 1)
-                high = jnp.where(here, x, high)
-            G[a, pl.ds(EDGE - SUB, SUB), :] = high[:SUB]
-            G[a, pl.ds(EDGE, fold), :] = low[:fold]
-            G[a, pl.ds(EDGE + fold, fold), :] = high[SUB:]
-            G[a, pl.ds(EDGE + nt, SUB), :] = low[fold:]
-        parts = [(c, n_seam) for c in range(outer_cols, outer_cols + wide, n_seam)]
-        for c, n in parts:
+                x = E[s, :, :]
+                if s != a:
+                    x = pltpu.roll(x, (s - a) * per % LANES, 1)
+                packed = jnp.where((lane >= s * per) & (lane < (s + 1) * per), x, packed)
+            G[a, pl.ds(outer_cols, wide), :] = packed
+        for c, n in tiles:
             at, at_before, at_after = pl.ds(c, n), pl.ds(c - 1, n), pl.ds(c + 1, n)
             rho = G[0, at, :]
             vel = [G[1 + a, at, :] for a in range(3)]
             inv_r, az_scale, width = (spread(seam_ref[g], n) for g in (0, 1, 2))
             dx = [seam_above(v) - seam_below(v) for v in vel]
-            dr = [seam_rise(v) * (0.5 / STEP_RADIAL) for v in vel]
+            dr = [seam_slope(v) for v in vel]
             dt = [(G[1 + a, at_after, :] - G[1 + a, at_before, :]) * az_scale for a in range(3)]
             dev, size = strain(dx, dr, dt, vel[1], vel[2], inv_r)
             scale = rho * width * size
-            for a in range(6):
-                GM[a, at, :] = seam_axial(scale * dev[a])
+            for q, a in enumerate(KEPT):
+                GM[q, at, :] = seam_axial(scale * dev[a])
             mom = [rho * v for v in vel]
             GH[0, at, :] = seam_axial(rho)
             for a in range(3):
                 GH[1 + a, at, :] = seam_axial(mom[a])
-            for q, (a, b) in enumerate(PAIRS):
-                GP[q, at, :] = seam_axial(mom[a] * vel[b])
-        for c, n in parts:
+            for q, p in enumerate(pairs(mom, vel)):
+                GP[q, at, :] = seam_axial(p)
+        for c, n in tiles:
             at = pl.ds(c, n)
-            hat = []
+            hat = [seam_radial(seam_turn(GH, a, c, n)) for a in range(4)]
+            inv = 1.0 / hat[0]
             for a in range(4):
-                s = seam_turn(GH, a, c, n)
-                GX[a, at, :] = s
-                hat.append(((pltpu.roll(s, 1, 1) + pltpu.roll(s, LANES - 1, 1)) + (s + s)) * (1.0 / 64.0))
-            inv = 1.0 / hat[0]
+                GHM[a, at, :] = hat[a]
             for a in range(3):
                 GV[a, at, :] = hat[1 + a] * inv
-            for a in range(6):
-                GX[4 + a, at, :] = seam_turn(GP, a, c, n)
-                GX[10 + a, at, :] = seam_turn(GM, a, c, n)
-
-    end_lane = pick(LANES - 1, 0)
-
-    def seam_end(x, ref, a, first, r):
-        shift = pick(LANES - 1 - SEAM // 2, LANES - SEAM // 2 + 1) - SEAM * (r + nx)
-        g = pltpu.roll(ref[a, pl.ds(first, x.shape[0]), :], shift, 1)
-        return jnp.where(lane_of(x) == end_lane, g, x)
-
-    def seam_slope(x, ref, a, first, r):
-        lo, hi = sides(x, seam_end(x, ref, a, first, r))
-        return hi - lo
-
-    def smooth(ref, a, row, first, n, at, r):
+        sums = [0.0, 0.0]
+        for c, n in inner:
+            at, at_before, at_after = pl.ds(c, n), pl.ds(c - 1, n), pl.ds(c + 1, n)
+            inv_r, az_scale, width4 = (spread(seam_ref[g], n) for g in (0, 1, 3))
+            hv = [GV[a, at, :] for a in range(3)]
+            dx = [seam_above(v) - seam_below(v) for v in hv]
+            dr = [seam_slope(v) for v in hv]
+            dt = [(GV[a, at_after, :] - GV[a, at_before, :]) * az_scale for a in range(3)]
+            dev, size = strain(dx, dr, dt, hv[1], hv[2], inv_r)
+            terms = contractions(
+                dev, width4 * GHM[0, at, :] * size,
+                [seam_radial(seam_turn(GP, q, c, n)) for q in range(5)],
+                [seam_radial(seam_turn(GM, q, c, n)) for q in range(5)],
+                [GHM[1 + a, at, :] for a in range(3)], hv)
+            sums = [x + fold_rows(y) for x, y in zip(sums, terms)]
+        for q in range(2):
+            row = jnp.sum(sums[q], axis=0, keepdims=True)
+            for r in range(pr):
+                shift = LANES - SEAM // 2 - SEAM * (nx + r)
+                SP[r, pl.ds(q, 1), :] = pltpu.roll(row, shift % LANES, 1)
+
+    def smooth(ref, a, row, first, n):
         x = ref[a, row, pl.ds(first, n), :]
         s = (ref[a, row, pl.ds(first - 1, n), :] + ref[a, row, pl.ds(first + 1, n), :]) + (x + x)
-        lo, hi = sides(s, seam_end(s, GX, at, first, r))
-        return ((lo + hi) + (s + s)) * (1.0 / 64.0)
+        return radial(s)
+
+    def whole_slope(a, x, first, r):
+        shift = pick(LANES - 1, LANES + 1) - SEAM // 2 - SEAM * (r + nx)
+        end = pick(LANES - 1, 0)
+        far = pltpu.roll(G[1 + a, pl.ds(first, x.shape[0]), :], shift, 1)
+        lane = lane_of(x)
+        far = jnp.where(lane == end, far, x)
+        lo = jnp.where(lane == 0, far, pltpu.roll(x, 1, 1))
+        hi = jnp.where(lane == LANES - 1, far, pltpu.roll(x, LANES - 1, 1))
+        return (hi - lo) * (0.5 / STEP_RADIAL)
 
     def low(r):
         return jnp.maximum(r - 1, jnp.where(pair_lo, -2, 0))
@@ -408,7 +451,7 @@
     def turn_slope(ref, a, row, first, n):
         return ref[a, row, pl.ds(first + 1, n), :] - ref[a, row, pl.ds(first - 1, n), :]
 
-    def first_pass(r, with_pairs):
+    def first_pass(r, with_pairs, exact):
         n = math.gcd(BLOCKS["first"], wide)
         for c in range(outer_cols, outer_cols + wide, n):
             rows = (low(r) + 2, r + 2, high(r) + 2)
@@ -416,7 +459,7 @@
             vel = [[S[1 + a, q, pl.ds(c, n), :] for a in range(3)] for q in rows]
             inv_r, az_scale, width = (spread(geo_ref[g, mine], n) for g in (0, 1, 2))
             dx = [vel[2][a] - vel[0][a] for a in range(3)]
-            dr = [seam_slope(vel[1][a], G, 1 + a, c, r) * (0.5 / STEP_RADIAL) for a in range(3)]
+            dr = [whole_slope(a, vel[1][a], c, r) if exact else slope(vel[1][a]) for a in range(3)]
             dt = [turn_slope(S, 1 + a, r + 2, c, n) * az_scale for a in range(3)]
             dev, size = strain(dx, dr, dt, vel[1][1], vel[1][2], inv_r)
             scale = rho[1] * width * size
@@ -427,14 +470,13 @@
             for a in range(3):
                 H[1 + a, r + 1, pl.ds(c, n), :] = (mom[0][a] + mom[1][a]) + (mom[1][a] + mom[2][a])
             if with_pairs:
-                for at, (a, b) in enumerate(PAIRS):
-                    p = [mom[q][a] * vel[q][b] for q in range(3)]
+                for at, p in enumerate(zip(*(pairs(mom[q], vel[q]) for q in range(3)))):
                     PX[at, r, pl.ds(c, n), :] = (p[0] + p[1]) + (p[1] + p[2])
 
     def hat_pass(r):
         n = math.gcd(BLOCKS["hat"], wide)
         for c in range(outer_cols, outer_cols + wide, n):
-            hat = [smooth(H, a, r + 1, c, n, a, r) for a in range(4)]
+            hat = [smooth(H, a, r + 1, c, n) for a in range(4)]
             inv = 1.0 / hat[0]
             for a in range(4):
                 HM[a, r + 1, pl.ds(c, n), :] = hat[a]
@@ -444,10 +486,10 @@
     def model_pass(r):
         n = math.gcd(BLOCKS["model"], wide)
         for c in range(outer_cols, outer_cols + wide, n):
-            for a in range(6):
+            for q, a in enumerate(KEPT):
                 x = M[mine, a, r + 1, pl.ds(c, n), :]
                 lo = M[mine, a, low(r) + 1, pl.ds(c, n), :]
-                MX[a, r, pl.ds(c, n), :] = (lo + x) + (x + M[mine, a, high(r) + 1, pl.ds(c, n), :])
+                MX[q, r, pl.ds(c, n), :] = (lo + x) + (x + M[mine, a, high(r) + 1, pl.ds(c, n), :])
 
     def closure_pass(r):
         sums = [0.0, 0.0]
@@ -457,32 +499,30 @@
             hv = [V[a, r + 1, pl.ds(c, n), :] for a in range(3)]
             hm = [HM[1 + a, r + 1, pl.ds(c, n), :] for a in range(3)]
             dx = [V[a, high(r) + 1, pl.ds(c, n), :] - V[a, low(r) + 1, pl.ds(c, n), :] for a in range(3)]
-            dr = [seam_slope(hv[a], GV, a, c, r) * (0.5 / STEP_RADIAL) for a in range(3)]
+            dr = [slope(hv[a]) for a in range(3)]
             dt = [turn_slope(V, a, r + 1, c, n) * az_scale for a in range(3)]
             dev, size = strain(dx, dr, dt, hv[1], hv[2], inv_r)
-            scale = width4 * HM[0, r + 1, pl.ds(c, n), :] * size
-            lm, mm = [], []
-            for at, (a, b) in enumerate(PAIRS):
-                mixed = scale * dev[at] - smooth(MX, at, r, c, n, 10 + at, r)
-                leonard = smooth(PX, at, r, c, n, 4 + at, r) - hm[a] * hv[b]
-                lm.append(leonard * mixed)
-                mm.append(mixed * mixed)
-            for q, terms in enumerate((lm, mm)):
-                diagonal, cross = (sum(terms[a] for a in group) for group in (DIAGONAL, CROSS))
-                cells = diagonal + 2.0 * cross
-                sums[q] += sum(cells[at:at + SUB] for at in range(0, n, SUB))
+            terms = contractions(
+                dev, width4 * HM[0, r + 1, pl.ds(c, n), :] * size,
+                [smooth(PX, q, r, c, n) for q in range(5)], [smooth(MX, q, r, c, n) for q in range(5)], hm, hv)
+            sums = [x + fold_rows(y) for x, y in zip(sums, terms)]
+        lane = lanes_at(1)
+        at_seam = jnp.where(odd == 0, LANES - 1 - lane, lane) < 2
         for q in range(2):
-            part[r, pl.ds(q, 1), :] = jnp.sum(sums[q], axis=0, keepdims=True)
+            row = jnp.sum(sums[q], axis=0, keepdims=True)
+            part[r, pl.ds(q, 1), :] = jnp.where(at_seam, SP[r, pl.ds(q, 1), :], row)
 
     def first_two(first, count, with_pairs=True):
-        sweep(first, count, lambda r: first_pass(r, with_pairs))
+        exact = min(max(nx + 1 - first, 0), count)
+        if exact:
+            sweep(first, exact, lambda r: first_pass(r, with_pairs, True))
+        if exact < count:
+            sweep(first + exact, count - exact, lambda r: first_pass(r, with_pairs, False))
         sweep(first, count, hat_pass)
 
     def close(first, count):
         sweep(first, count, model_pass)
         sweep(first, count, closure_pass)
-
-    seam_far = pick(LANES - 1, 1)
 
     def other_half(i):
         n = math.gcd(BLOCKS["other"], wide)
@@ -495,8 +535,11 @@
             dr = []
             for a in range(3):
                 far = pltpu.roll(S[1 + a, own_at + i, pl.ds(c, n), :], pick(1, LANES - 1), 1)
-                before_, after_ = sides(vel[a], jnp.where(lane_of(far) == pick(0, LANES - 1), far, vel[a]))
-                dr.append((after_ - before_) * (0.5 / STEP_RADIAL))
+                lane = lane_of(far)
+                end = jnp.where(lane == pick(0, LANES - 1), far, vel[a])
+                lo_side = jnp.where(lane == 0, end, pltpu.roll(vel[a], 1, 1))
+                hi_side = jnp.where(lane == LANES - 1, end, pltpu.roll(vel[a], LANES - 1, 1))
+                dr.append((hi_side - lo_side) * (0.5 / STEP_RADIAL))
             dt = [turn_slope(T, 1 + a, i + 1, c, n) * az_scale for a in range(3)]
             dev, size = strain(dx, dr, dt, vel[1], vel[2], inv_r)
             scale = T[0, i + 1, pl.ds(c, n), :] * width * size
@@ -764,8 +807,8 @@
 
 def shards(n_ax, n_az, density, velocity):
     nx, nt, radial = density.shape
-    assert radial == 2 * LANES and 2 * 4 * nx * SEAM == LANES and n_ax % 2 == 0
-    pr, seam_rows = 2 * nx, nt // 2 + 2 * SUB
+    assert radial == 2 * LANES and 4 * nx * SEAM == LANES and n_ax % 2 == 0
+    pr, seam_rows = 2 * nx, nt + 2 * SUB
     halves, seam = geometry(radial, nt * n_az)
 
     def field(*lead):
@@ -798,15 +841,16 @@
             field(4, pr + 2),
             field(3, pr + 2),
             field(4, pr + 2),
-            field(6, pr),
-            field(6, pr),
+            field(5, pr),
+            field(5, pr),
             vmem(4, seam_rows, LANES),
             field(4),
-            field(6),
+            field(5),
             field(4),
-            field(6),
-            field(16),
+            field(5),
+            field(4),
             field(3),
+            vmem(pr, 2, LANES),
             vmem(pr, 2, LANES),
             vmem(2, n_az, pr, 2, LANES),
             vmem(2, n_az, 2, LANES),

time: 33.9 us -> 32.9 us (0.971)
  Pallas kernels: 33.2 us -> 32.1 us
    pallas_call x1, Pallas kernels: 32.2 us -> 31.2 us  [shards(): pl.pallas_call(functools.partial(kernel, n_ax, n_az, nx, nt), out_shape=(...]
where the time goes in v3:
time: 32.9 us; the launch traced here: 32.8 us
  Pallas kernels  32.1 us (98%)
  between operations  0.64 us (2%)
    pallas_call x1, Pallas kernels, shards(): pl.pallas_call(functools.partial(kernel, n_ax, n_az, nx, nt), out_shape=(...  31.2 us
    pallas_call x1, Pallas kernels, shards(): pl.pallas_call(hand_over, out_shape=(jax.ShapeDtypeStruct(flux.shape, jnp...  0.95 us

profile of v3, /device:TPU:0, one launch (start us, length us, event | category | flops | bytes accessed | tf_op | source)
XLA Modules:
  0.0 32.8 jit_solution(17256462940411529234)
XLA Ops:
  0.6 31.2 %closure.1 = (f32[3,4,64,256]{3,2,1,0:T(8,128)S(1)}, f32[4,256]{1,0:T(4,128)S(1)}) custom-call(f32[4,64,256]{2,1,0:T(8,128)} %rho_ref.1, f32[3,4,64,256]{3,2,1,0:T(8,128)} %vel_ref.1, f32[8,2,8,128]{3,2,1,0:T(8,128)} %constant.4.clone.geo_in, f32[4,8,128]{2,1,0:T(8,128)} %constant.5.clone.seam_in), custom_call_target="tpu_custom_call" | custom-call | tf_op jit(solution)/shard_map/closure/pallas_call | solution.py:821
  31.8 1.0 %hand_over.1 = (f32[3,4,64,256]{3,2,1,0:T(8,128)}, f32[4,256]{1,0:T(4,128)}) custom-call(f32[3,4,64,256]{3,2,1,0:T(8,128)S(1)} %get-tuple-element.4.flux_in, f32[4,256]{1,0:T(4,128)S(1)} %get-tuple-element.5.coef_in), custom_call_target="tpu_custom_call" | custom-call | tf_op jit(solution)/shard_map/hand_over/pallas_call | solution.py:871

commit v4 on v3

--- a/solution.py
+++ b/solution.py
@@ -451,37 +451,33 @@
     def turn_slope(ref, a, row, first, n):
         return ref[a, row, pl.ds(first + 1, n), :] - ref[a, row, pl.ds(first - 1, n), :]
 
-    def first_pass(r, with_pairs, exact):
-        n = math.gcd(BLOCKS["first"], wide)
-        for c in range(outer_cols, outer_cols + wide, n):
-            rows = (low(r) + 2, r + 2, high(r) + 2)
-            rho = [S[0, q, pl.ds(c, n), :] for q in rows]
-            vel = [[S[1 + a, q, pl.ds(c, n), :] for a in range(3)] for q in rows]
-            inv_r, az_scale, width = (spread(geo_ref[g, mine], n) for g in (0, 1, 2))
-            dx = [vel[2][a] - vel[0][a] for a in range(3)]
-            dr = [whole_slope(a, vel[1][a], c, r) if exact else slope(vel[1][a]) for a in range(3)]
-            dt = [turn_slope(S, 1 + a, r + 2, c, n) * az_scale for a in range(3)]
-            dev, size = strain(dx, dr, dt, vel[1][1], vel[1][2], inv_r)
-            scale = rho[1] * width * size
-            for a in range(6):
-                M[mine, a, r + 1, pl.ds(c, n), :] = scale * dev[a]
-            mom = [[rho[q] * vel[q][a] for a in range(3)] for q in range(3)]
-            H[0, r + 1, pl.ds(c, n), :] = (rho[0] + rho[1]) + (rho[1] + rho[2])
-            for a in range(3):
-                H[1 + a, r + 1, pl.ds(c, n), :] = (mom[0][a] + mom[1][a]) + (mom[1][a] + mom[2][a])
-            if with_pairs:
-                for at, p in enumerate(zip(*(pairs(mom[q], vel[q]) for q in range(3)))):
-                    PX[at, r, pl.ds(c, n), :] = (p[0] + p[1]) + (p[1] + p[2])
-
-    def hat_pass(r):
-        n = math.gcd(BLOCKS["hat"], wide)
-        for c in range(outer_cols, outer_cols + wide, n):
-            hat = [smooth(H, a, r + 1, c, n) for a in range(4)]
-            inv = 1.0 / hat[0]
-            for a in range(4):
-                HM[a, r + 1, pl.ds(c, n), :] = hat[a]
-            for a in range(3):
-                V[a, r + 1, pl.ds(c, n), :] = hat[1 + a] * inv
+    def first_block(r, with_pairs, exact, c, n):
+        rows = (low(r) + 2, r + 2, high(r) + 2)
+        rho = [S[0, q, pl.ds(c, n), :] for q in rows]
+        vel = [[S[1 + a, q, pl.ds(c, n), :] for a in range(3)] for q in rows]
+        inv_r, az_scale, width = (spread(geo_ref[g, mine], n) for g in (0, 1, 2))
+        dx = [vel[2][a] - vel[0][a] for a in range(3)]
+        dr = [whole_slope(a, vel[1][a], c, r) if exact else slope(vel[1][a]) for a in range(3)]
+        dt = [turn_slope(S, 1 + a, r + 2, c, n) * az_scale for a in range(3)]
+        dev, size = strain(dx, dr, dt, vel[1][1], vel[1][2], inv_r)
+        scale = rho[1] * width * size
+        for a in range(6):
+            M[mine, a, r + 1, pl.ds(c, n), :] = scale * dev[a]
+        mom = [[rho[q] * vel[q][a] for a in range(3)] for q in range(3)]
+        H[0, r + 1, pl.ds(c, n), :] = (rho[0] + rho[1]) + (rho[1] + rho[2])
+        for a in range(3):
+            H[1 + a, r + 1, pl.ds(c, n), :] = (mom[0][a] + mom[1][a]) + (mom[1][a] + mom[2][a])
+        if with_pairs:
+            for at, p in enumerate(zip(*(pairs(mom[q], vel[q]) for q in range(3)))):
+                PX[at, r, pl.ds(c, n), :] = (p[0] + p[1]) + (p[1] + p[2])
+
+    def hat_block(r, c, n):
+        hat = [smooth(H, a, r + 1, c, n) for a in range(4)]
+        inv = 1.0 / hat[0]
+        for a in range(4):
+            HM[a, r + 1, pl.ds(c, n), :] = hat[a]
+        for a in range(3):
+            V[a, r + 1, pl.ds(c, n), :] = hat[1 + a] * inv
 
     def model_pass(r):
         n = math.gcd(BLOCKS["model"], wide)
@@ -513,12 +509,22 @@
             part[r, pl.ds(q, 1), :] = jnp.where(at_seam, SP[r, pl.ds(q, 1), :], row)
 
     def first_two(first, count, with_pairs=True):
+        n = math.gcd(BLOCKS["first"], wide)
+        blocks = list(range(outer_cols, outer_cols + wide, n))
+
+        def both(exact, r):
+            for at, c in enumerate(blocks):
+                first_block(r, with_pairs, exact, c, n)
+                if at >= 2:
+                    hat_block(r, blocks[at - 2], n)
+            for c in blocks[-2:]:
+                hat_block(r, c, n)
+
         exact = min(max(nx + 1 - first, 0), count)
         if exact:
-            sweep(first, exact, lambda r: first_pass(r, with_pairs, True))
+            sweep(first, exact, functools.partial(both, True))
         if exact < count:
-            sweep(first + exact, count - exact, lambda r: first_pass(r, with_pairs, False))
-        sweep(first, count, hat_pass)
+            sweep(first + exact, count - exact, functools.partial(both, False))
 
     def close(first, count):
         sweep(first, count, model_pass)
@@ -557,12 +563,17 @@
         c.wait()
     pack_seam()
     pl.semaphore_wait(barrier, peers)
-    start([seam_swap] + swap_ends)
-    start(seam_own + own_around)
-
-    @pl.when(has_near)
-    def _():
-        start([seam_near] + near_ends + near_rows)
+    seam_swap.start()
+
+    @pl.when(has_near)
+    def _():
+        seam_near.start()
+
+    start(swap_ends + seam_own + own_around)
+
+    @pl.when(has_near)
+    def _():
+        start(near_ends + near_rows)
 
     for q in [nx - 1, nx - 2] + list(range(nx - 2)):
         start(swap_rows[q])
@@ -614,21 +625,31 @@
         arrive(pass_ends)
         start(ahead_around)
 
-    for at in range(2):
+    def hand_on(at):
         arrive(swap_rows[nx - 1 - at])
 
         @pl.when(has_far)
         def _():
             pass_rows[at].start()
 
+    hand_on(0)
+
     @pl.when(has_far)
     def _():
-        arrive(near_rows)
-        arrive(beyond_around)
+        arrive(near_rows + beyond_around)
 
     arrive(partner_around)
+    first_two(pr, 1, False)
+    hand_on(1)
     first_two(pr - 1, 1)
-    first_two(pr, 1, False)
+
+    @pl.when(has_near)
+    def _():
+        edge_vel.start()
+        arrive([pass_rows[0]] + ahead_around)
+
+    first_two(0, 1)
+    close(1, 1)
     for q in range(nx - 3):
         arrive(swap_rows[q])
         first_two(nx - 1 + q, 1)
@@ -636,13 +657,10 @@
 
     @pl.when(has_near)
     def _():
-        edge_vel.start()
-        arrive(pass_rows)
-        arrive(ahead_around)
+        arrive([pass_rows[1]])
 
     first_two(-1, 1, False)
-    first_two(0, 1)
-    close(0, 2)
+    close(0, 1)
     arrive(swap_rows[nx - 3])
     swap_stress.start()
 

time: 32.9 us -> 31.9 us (0.970)
  Pallas kernels: 32.1 us -> 31.1 us
    pallas_call x1, Pallas kernels: 31.2 us -> 30.2 us  [shards(): pl.pallas_call(functools.partial(kernel, n_ax, n_az, nx, nt), out_shape=(...]
where the time goes in v4:
time: 31.9 us; the launch traced here: 31.8 us
  Pallas kernels  31.1 us (97%)
  between operations  0.64 us (2%)
    pallas_call x1, Pallas kernels, shards(): pl.pallas_call(functools.partial(kernel, n_ax, n_az, nx, nt), out_shape=(...  30.2 us
    pallas_call x1, Pallas kernels, shards(): pl.pallas_call(hand_over, out_shape=(jax.ShapeDtypeStruct(flux.shape, jnp...  0.95 us

profile of v4, /device:TPU:0, one launch (start us, length us, event | category | flops | bytes accessed | tf_op | source)
XLA Modules:
  0.0 31.8 jit_solution(11076611939435008281)
XLA Ops:
  0.6 30.2 %closure.1 = (f32[3,4,64,256]{3,2,1,0:T(8,128)S(1)}, f32[4,256]{1,0:T(4,128)S(1)}) custom-call(f32[4,64,256]{2,1,0:T(8,128)} %rho_ref.1, f32[3,4,64,256]{3,2,1,0:T(8,128)} %vel_ref.1, f32[8,2,8,128]{3,2,1,0:T(8,128)} %constant.4.clone.geo_in, f32[4,8,128]{2,1,0:T(8,128)} %constant.5.clone.seam_in), custom_call_target="tpu_custom_call" | custom-call | tf_op jit(solution)/shard_map/closure/pallas_call | solution.py:839
  30.8 1.0 %hand_over.1 = (f32[3,4,64,256]{3,2,1,0:T(8,128)}, f32[4,256]{1,0:T(4,128)}) custom-call(f32[3,4,64,256]{3,2,1,0:T(8,128)S(1)} %get-tuple-element.4.flux_in, f32[4,256]{1,0:T(4,128)S(1)} %get-tuple-element.5.coef_in), custom_call_target="tpu_custom_call" | custom-call | tf_op jit(solution)/shard_map/hand_over/pallas_call | solution.py:889

commit v5 on v4

--- a/solution.py
+++ b/solution.py
@@ -94,9 +94,8 @@
     return [mom[a] * vel[a] - azimuthal for a in (0, 1)] + [mom[a] * vel[b] for a, b in CROSS]
 
 
-def contractions(dev, scale, hat_pairs, hat_model, hat_mom, hat_vel):
+def contractions(dev, scale, leonard, hat_model):
     mixed = [scale * dev[a] - m for a, m in zip(KEPT, hat_model)]
-    leonard = [p - q for p, q in zip(hat_pairs, pairs(hat_mom, hat_vel))]
 
     def cross(left, right):
         return 2.0 * (left[2] * right[2] + left[3] * right[3] + left[4] * right[4])
@@ -133,7 +132,7 @@
 def kernel(
     n_ax, n_az, nx, nt,
     rho_ref, vel_ref, geo_in, seam_in, flux_ref, coef_ref,
-    S, T, M, H, V, HM, PX, MX, E, G, GM, GH, GP, GHM, GV, SP,
+    S, T, M, H, V, HM, PX, MX, LE, E, G, GM, GH, GP, GHM, GV, SP,
     part, rec, rec_out, CS, geo_ref, seam_ref, own_sem, send_sem, recv_sem, sum_send, sum_recv,
 ):
     pr = 2 * nx
@@ -409,9 +408,9 @@
             dev, size = strain(dx, dr, dt, hv[1], hv[2], inv_r)
             terms = contractions(
                 dev, width4 * GHM[0, at, :] * size,
-                [seam_radial(seam_turn(GP, q, c, n)) for q in range(5)],
-                [seam_radial(seam_turn(GM, q, c, n)) for q in range(5)],
-                [GHM[1 + a, at, :] for a in range(3)], hv)
+                [seam_radial(seam_turn(GP, q, c, n)) - p for q, p in
+                 enumerate(pairs([GHM[1 + a, at, :] for a in range(3)], hv))],
+                [seam_radial(seam_turn(GM, q, c, n)) for q in range(5)])
             sums = [x + fold_rows(y) for x, y in zip(sums, terms)]
         for q in range(2):
             row = jnp.sum(sums[q], axis=0, keepdims=True)
@@ -440,9 +439,9 @@
     def high(r):
         return jnp.minimum(r + 1, jnp.where(pair_hi, pr + 1, pr - 1))
 
-    def sweep(first, count, body):
+    def sweep(first, count, body, stride=1):
         def step(at, carry):
-            t = first + at
+            t = first + at * stride
             body(pick(t, pr - 1 - t))
             return carry
 
@@ -487,20 +486,27 @@
                 lo = M[mine, a, low(r) + 1, pl.ds(c, n), :]
                 MX[q, r, pl.ds(c, n), :] = (lo + x) + (x + M[mine, a, high(r) + 1, pl.ds(c, n), :])
 
+    def leonard_pass(r):
+        n = math.gcd(BLOCKS["closure"], nt)
+        for c in range(EDGE, EDGE + nt, n):
+            hv = [V[a, r + 1, pl.ds(c, n), :] for a in range(3)]
+            hm = [HM[1 + a, r + 1, pl.ds(c, n), :] for a in range(3)]
+            for q, p in enumerate(pairs(hm, hv)):
+                LE[q, r, pl.ds(c, n), :] = smooth(PX, q, r, c, n) - p
+
     def closure_pass(r):
         sums = [0.0, 0.0]
         n = math.gcd(BLOCKS["closure"], nt)
         for c in range(EDGE, EDGE + nt, n):
             inv_r, az_scale, width4 = (spread(geo_ref[g, mine], n) for g in (0, 1, 3))
             hv = [V[a, r + 1, pl.ds(c, n), :] for a in range(3)]
-            hm = [HM[1 + a, r + 1, pl.ds(c, n), :] for a in range(3)]
             dx = [V[a, high(r) + 1, pl.ds(c, n), :] - V[a, low(r) + 1, pl.ds(c, n), :] for a in range(3)]
             dr = [slope(hv[a]) for a in range(3)]
             dt = [turn_slope(V, a, r + 1, c, n) * az_scale for a in range(3)]
             dev, size = strain(dx, dr, dt, hv[1], hv[2], inv_r)
             terms = contractions(
                 dev, width4 * HM[0, r + 1, pl.ds(c, n), :] * size,
-                [smooth(PX, q, r, c, n) for q in range(5)], [smooth(MX, q, r, c, n) for q in range(5)], hm, hv)
+                [LE[q, r, pl.ds(c, n), :] for q in range(5)], [smooth(MX, q, r, c, n) for q in range(5)])
             sums = [x + fold_rows(y) for x, y in zip(sums, terms)]
         lane = lanes_at(1)
         at_seam = jnp.where(odd == 0, LANES - 1 - lane, lane) < 2
@@ -526,9 +532,14 @@
         if exact < count:
             sweep(first + exact, count - exact, functools.partial(both, False))
 
-    def close(first, count):
-        sweep(first, count, model_pass)
-        sweep(first, count, closure_pass)
+    def close(first, count, stride=1, leonard=True):
+        def both(r):
+            if leonard:
+                leonard_pass(r)
+            model_pass(r)
+            closure_pass(r)
+
+        sweep(first, count, both, stride)
 
     def other_half(i):
         n = math.gcd(BLOCKS["other"], wide)
@@ -642,6 +653,7 @@
     first_two(pr, 1, False)
     hand_on(1)
     first_two(pr - 1, 1)
+    sweep(pr - 1, 1, leonard_pass)
 
     @pl.when(has_near)
     def _():
@@ -654,6 +666,7 @@
         arrive(swap_rows[q])
         first_two(nx - 1 + q, 1)
         close(nx - 2 + q, 1)
+    sweep(pr - 5, 1, leonard_pass)
 
     @pl.when(has_near)
     def _():
@@ -669,7 +682,8 @@
         edge_stress.start()
 
     first_two(pr - 4, 3)
-    close(pr - 5, 5)
+    close(pr - 4, 3)
+    close(pr - 5, 2, 4, False)
 
     def share(at, src, dst, ax, d):
         return pltpu.make_async_remote_copy(
@@ -688,16 +702,17 @@
     down, up = end_row(0, mine, 0, lower_ax), end_row(1, mine, pr - 1, upper_ax)
     end_sums = end_row(even, 0, 0, me_ax) + end_row(even, 1, 0, me_ax)
 
-    @pl.when(pair_lo)
-    def _():
-        start(down)
-
-    @pl.when(pair_hi)
-    def _():
-        start(up)
-
     start(over)
     start(across)
+
+    @pl.when(pair_lo)
+    def _():
+        start(down)
+
+    @pl.when(pair_hi)
+    def _():
+        start(up)
+
     rec[mine, me_az] = part[...]
     swap_vel.wait_recv()
     start(swap_vel_around)
@@ -859,6 +874,7 @@
             field(4, pr + 2),
             field(3, pr + 2),
             field(4, pr + 2),
+            field(5, pr),
             field(5, pr),
             field(5, pr),
             vmem(4, seam_rows, LANES),

time: 31.9 us -> 31.4 us (0.984)
  Pallas kernels: 31.1 us -> 30.6 us
    pallas_call x1, Pallas kernels: 30.2 us -> 29.7 us  [shards(): pl.pallas_call(functools.partial(kernel, n_ax, n_az, nx, nt), out_shape=(...]
where the time goes in v5:
time: 31.4 us; the launch traced here: 31.3 us
  Pallas kernels  30.6 us (97%)
  between operations  0.64 us (2%)
    pallas_call x1, Pallas kernels, shards(): pl.pallas_call(functools.partial(kernel, n_ax, n_az, nx, nt), out_shape=(...  29.7 us
    pallas_call x1, Pallas kernels, shards(): pl.pallas_call(hand_over, out_shape=(jax.ShapeDtypeStruct(flux.shape, jnp...  0.95 us

profile of v5, /device:TPU:0, one launch (start us, length us, event | category | flops | bytes accessed | tf_op | source)
XLA Modules:
  0.0 31.3 jit_solution(6575641446423935455)
XLA Ops:
  0.6 29.7 %closure.1 = (f32[3,4,64,256]{3,2,1,0:T(8,128)S(1)}, f32[4,256]{1,0:T(4,128)S(1)}) custom-call(f32[4,64,256]{2,1,0:T(8,128)} %rho_ref.1, f32[3,4,64,256]{3,2,1,0:T(8,128)} %vel_ref.1, f32[8,2,8,128]{3,2,1,0:T(8,128)} %constant.4.clone.geo_in, f32[4,8,128]{2,1,0:T(8,128)} %constant.5.clone.seam_in), custom_call_target="tpu_custom_call" | custom-call | tf_op jit(solution)/shard_map/closure/pallas_call | solution.py:854
  30.3 1.0 %hand_over.1 = (f32[3,4,64,256]{3,2,1,0:T(8,128)}, f32[4,256]{1,0:T(4,128)}) custom-call(f32[3,4,64,256]{3,2,1,0:T(8,128)S(1)} %get-tuple-element.4.flux_in, f32[4,256]{1,0:T(4,128)S(1)} %get-tuple-element.5.coef_in), custom_call_target="tpu_custom_call" | custom-call | tf_op jit(solution)/shard_map/hand_over/pallas_call | solution.py:905

commit v6 on v5

--- a/solution.py
+++ b/solution.py
@@ -22,7 +22,7 @@
 EDGE = 16
 SEAM = 8
 COPIES = 64
-BLOCKS = {'first': 16, 'hat': 16, 'model': 16, 'closure': 16, 'other': 16, 'flux': 16, 'seam': 16}
+BLOCKS = {'first': 8, 'hat': 16, 'model': 16, 'closure': 16, 'other': 16, 'flux': 8, 'seam': 16}
 MESH_ID = pl.DeviceIdType.MESH
 
 
@@ -423,10 +423,13 @@
         s = (ref[a, row, pl.ds(first - 1, n), :] + ref[a, row, pl.ds(first + 1, n), :]) + (x + x)
         return radial(s)
 
-    def whole_slope(a, x, first, r):
+    def whole_slope(a, x, first, r, held):
         shift = pick(LANES - 1, LANES + 1) - SEAM // 2 - SEAM * (r + nx)
         end = pick(LANES - 1, 0)
-        far = pltpu.roll(G[1 + a, pl.ds(first, x.shape[0]), :], shift, 1)
+        if held:
+            far = pltpu.roll(T[1 + a, r - own_row + 1, pl.ds(first, x.shape[0]), :], pick(LANES - 1, 1), 1)
+        else:
+            far = pltpu.roll(G[1 + a, pl.ds(first, x.shape[0]), :], shift, 1)
         lane = lane_of(x)
         far = jnp.where(lane == end, far, x)
         lo = jnp.where(lane == 0, far, pltpu.roll(x, 1, 1))
@@ -450,13 +453,13 @@
     def turn_slope(ref, a, row, first, n):
         return ref[a, row, pl.ds(first + 1, n), :] - ref[a, row, pl.ds(first - 1, n), :]
 
-    def first_block(r, with_pairs, exact, c, n):
+    def first_block(r, with_pairs, exact, held, c, n):
         rows = (low(r) + 2, r + 2, high(r) + 2)
         rho = [S[0, q, pl.ds(c, n), :] for q in rows]
         vel = [[S[1 + a, q, pl.ds(c, n), :] for a in range(3)] for q in rows]
         inv_r, az_scale, width = (spread(geo_ref[g, mine], n) for g in (0, 1, 2))
         dx = [vel[2][a] - vel[0][a] for a in range(3)]
-        dr = [whole_slope(a, vel[1][a], c, r) if exact else slope(vel[1][a]) for a in range(3)]
+        dr = [whole_slope(a, vel[1][a], c, r, held) if exact else slope(vel[1][a]) for a in range(3)]
         dt = [turn_slope(S, 1 + a, r + 2, c, n) * az_scale for a in range(3)]
         dev, size = strain(dx, dr, dt, vel[1][1], vel[1][2], inv_r)
         scale = rho[1] * width * size
@@ -514,13 +517,13 @@
             row = jnp.sum(sums[q], axis=0, keepdims=True)
             part[r, pl.ds(q, 1), :] = jnp.where(at_seam, SP[r, pl.ds(q, 1), :], row)
 
-    def first_two(first, count, with_pairs=True):
+    def first_two(first, count, with_pairs=True, held=False):
         n = math.gcd(BLOCKS["first"], wide)
         blocks = list(range(outer_cols, outer_cols + wide, n))
 
         def both(exact, r):
             for at, c in enumerate(blocks):
-                first_block(r, with_pairs, exact, c, n)
+                first_block(r, with_pairs, exact, held, c, n)
                 if at >= 2:
                     hat_block(r, blocks[at - 2], n)
             for c in blocks[-2:]:
@@ -609,6 +612,7 @@
         seam_pass.wait_recv()
         start(seam_ahead_around)
 
+    first_two(1, nx - 2, held=True)
     arrive(swap_ends)
     start(partner_around)
 
@@ -629,7 +633,6 @@
         arrive(seam_ahead_around)
 
     seam_pass_all()
-    first_two(1, nx - 2)
 
     @pl.when(has_near)
     def _():

time: 31.4 us -> 31.3 us (level); the launches traced: 31.3 us -> 30.8 us
  Pallas kernels: 30.6 us -> 30.2 us
    pallas_call x1, Pallas kernels: 29.7 us -> 29.2 us  [shards(): pl.pallas_call(functools.partial(kernel, n_ax, n_az, nx, nt), out_shape=(...]
where the time goes in v6:
time: 31.3 us; the launch traced here: 30.8 us
  Pallas kernels  30.2 us (96%)
  between operations  0.64 us (2%)
    pallas_call x1, Pallas kernels, shards(): pl.pallas_call(functools.partial(kernel, n_ax, n_az, nx, nt), out_shape=(...  29.2 us
    pallas_call x1, Pallas kernels, shards(): pl.pallas_call(hand_over, out_shape=(jax.ShapeDtypeStruct(flux.shape, jnp...  0.95 us

profile of v6, /device:TPU:0, one launch (start us, length us, event | category | flops | bytes accessed | tf_op | source)
XLA Modules:
  0.0 30.8 jit_solution(11404438289969454)
XLA Ops:
  0.6 29.2 %closure.1 = (f32[3,4,64,256]{3,2,1,0:T(8,128)S(1)}, f32[4,256]{1,0:T(4,128)S(1)}) custom-call(f32[4,64,256]{2,1,0:T(8,128)} %rho_ref.1, f32[3,4,64,256]{3,2,1,0:T(8,128)} %vel_ref.1, f32[8,2,8,128]{3,2,1,0:T(8,128)} %constant.4.clone.geo_in, f32[4,8,128]{2,1,0:T(8,128)} %constant.5.clone.seam_in), custom_call_target="tpu_custom_call" | custom-call | tf_op jit(solution)/shard_map/closure/pallas_call | solution.py:857
  29.9 1.0 %hand_over.1 = (f32[3,4,64,256]{3,2,1,0:T(8,128)}, f32[4,256]{1,0:T(4,128)}) custom-call(f32[3,4,64,256]{3,2,1,0:T(8,128)S(1)} %get-tuple-element.4.flux_in, f32[4,256]{1,0:T(4,128)S(1)} %get-tuple-element.5.coef_in), custom_call_target="tpu_custom_call" | custom-call | tf_op jit(solution)/shard_map/hand_over/pallas_call | solution.py:908
